TPU v7x, 32 devices: a whole 2x2x4 slice. The times are simulated.
32 devices in a mesh: gx: 8 (over z, y), gy: 2 (over x), gz: 2 (over core).
Axes of the slice: x: 2, y: 2, z: 4, core: 2. Of those that a mesh axis runs over, the one named last changes fastest.
Arguments:
- populations: float32 [19, 64, 32, 256], P(None, 'gx', 'gy', 'gz'), as said below
- coarse_pops: float32 [19, 32, 16, 128], P(None, 'gx', 'gy', 'gz'), as said below
- fine_mask: int32 [64, 32, 256], P('gx', 'gy', 'gz'), may hold values 0 or 1
- coarse_mask: int32 [32, 16, 128], P('gx', 'gy', 'gz'), may hold values 0 or 1
- bead_data: float32 [8, 2, 2, 6, 512], P('gx', 'gy', 'gz'), as said below
- bead_bins: int32 [8, 2, 2, 1, 512], P('gx', 'gy', 'gz'), may hold values from -1 to 127, as said below
Outputs:
- fine_out: float32 [19, 64, 32, 256], P(None, 'gx', 'gy', 'gz')
- coarse_out: float32 [19, 32, 16, 128], P(None, 'gx', 'gy', 'gz')
Inputs may be any that keep to these rules, and one draw needn't show every extreme that they name: `populations`: populations are positive; rest population near 1/3, axis ones near 1/18, edge ones near 1/36, density within 0.5 to 1.7. `coarse_pops`: same law as populations on the coarse grid. `bead_bins`: in each source's block of 32 slots for one owner, the live slots come first; one owner receives 32 live slots from every source in every draw. `bead_data`: row 0 and 1 lie in -0.5 to 1.5, row 2 in -0.5 to 32 - 0.5; values in empty slots are arbitrary.
All inputs are finite; a program needn't handle non-finite values. No bound on the sum of `fine_mask` or of `coarse_mask` on one device may be relied on, other than what follows from the above.
Results may differ from a plain program's by a relative error of at most 0.0003.
Values sent between devices are 32-bit elements; how exact they have to be, the bound alone decides.
A program may use at most 128 MiB of HBM per device.

v0:
```python
import functools

import jax
import jax.numpy as jnp
import numpy as np
from jax import lax
from jax.experimental import pallas as pl
from jax.experimental.pallas import tpu as pltpu
from jax.sharding import PartitionSpec as P

BIN_Z = 32
VELOCITIES = [
    (0, 0, 0), (1, 0, 0), (-1, 0, 0), (0, 1, 0), (0, -1, 0), (0, 0, 1), (0, 0, -1),
    (1, 1, 0), (-1, -1, 0), (1, -1, 0), (-1, 1, 0), (1, 0, 1), (-1, 0, -1), (1, 0, -1),
    (-1, 0, 1), (0, 1, 1), (0, -1, -1), (0, 1, -1), (0, -1, 1),
]
WEIGHTS = [1.0 / 3.0] + [1.0 / 18.0] * 6 + [1.0 / 36.0] * 12
TAU_FINE = 1.2
TAU_COARSE = 0.85
TO_COARSE = 2.0 * TAU_COARSE / TAU_FINE
TO_FINE = TAU_FINE / (2.0 * TAU_COARSE)
LANES = 128
LIMIT = 24 * 2**20
MESH = pl.DeviceIdType.MESH
SIGNS = (1, -1)
FACE = {(a, s): [i for i in range(19) if VELOCITIES[i][a] == s] for a in range(3) for s in SIGNS}
FACES = [(a, s) for a in range(3) for s in SIGNS]
EDGES = [i for i in range(7, 19)]


def along(vector, c):
    total = None
    for part, sign in zip(vector, c):
        if sign:
            total = part if total is None else (total + part if sign > 0 else total - part)
    return total


def moments(p):
    rho = p[0]
    sums = [None] * 19
    m = [None] * 3
    for i in range(1, 19, 2):
        rho = rho + (p[i] + p[i + 1])
        sums[i] = p[i] - p[i + 1]
        for axis, sign in enumerate(VELOCITIES[i]):
            if sign:
                if m[axis] is None:
                    m[axis] = sums[i]
                else:
                    m[axis] = m[axis] + sums[i] if sign > 0 else m[axis] - sums[i]
    return rho, m


def relax(p, rho, u, a, b, force=None, k=0.0):
    scaled = b * rho
    base = scaled * (1.0 - 1.5 * (u[0] * u[0] + u[1] * u[1] + u[2] * u[2]))
    lin = [3.0 * scaled * v for v in u]
    quad = [4.5 * scaled * v for v in u]
    if force is not None:
        base = base - (3.0 * k) * (u[0] * force[0] + u[1] * force[1] + u[2] * force[2])
        lin = [v + (3.0 * k) * f for v, f in zip(lin, force)]
        quad = [v + (9.0 * k) * f for v, f in zip(quad, force)]
    out = [None] * 19
    out[0] = a * p[0] + WEIGHTS[0] * base
    for i in range(1, 19, 2):
        c, w = VELOCITIES[i], WEIGHTS[i]
        even = w * (base + along(u, c) * along(quad, c))
        odd = w * along(lin, c)
        out[i] = a * p[i] + (even + odd)
        out[i + 1] = a * p[i + 1] + (even - odd)
    return out


def parts(x):
    high = x.astype(jnp.bfloat16)
    return high, (x - high.astype(jnp.float32)).astype(jnp.bfloat16)


def times_exact(x, table):
    high, low = parts(x)
    dot = functools.partial(jnp.dot, preferred_element_type=jnp.float32)
    return dot(high, table) + dot(low, table)


def moved(plane, c):
    rows, lanes = plane.shape
    if c[1]:
        plane = pltpu.roll(plane, 1 if c[1] > 0 else rows - 1, 0)
    if c[2]:
        plane = pltpu.roll(plane, 1 if c[2] > 0 else lanes - 1, 1)
    return plane


def side(sign, length):
    return 0 if sign > 0 else length - 1


def slot_of(sign):
    return 0 if sign > 0 else 1


def pack_x(target, xs, es):
    _, fx, fy, fz = target.shape
    row = lax.broadcasted_iota(jnp.int32, (fy, LANES), 0)
    diagonal = row == lax.broadcasted_iota(jnp.int32, (fy, LANES), 1)
    for s in SIGNS:
        for j, i in enumerate(FACE[0, s]):
            plane = target[i, side(s, fx)]
            xs[slot_of(s), j] = plane
            c = VELOCITIES[i]
            if c[1]:
                y = side(c[1], fy)
                es[EDGES.index(i), :, 0:fz] = plane[y : y + 1]
            elif c[2]:
                z = side(c[2], fz)
                turned = jnp.where(diagonal, plane[:, z : z + 1], 0.0)
                es[EDGES.index(i)] = jnp.sum(turned, axis=0, keepdims=True)


def pack_yz(target, ys, zs, es):
    _, fx, fy, fz = target.shape
    lane = lax.broadcasted_iota(jnp.int32, (fy, LANES), 1)
    for s in SIGNS:
        y, z = side(s, fy), side(s, fz)
        for j, i in enumerate(FACE[1, s]):
            for x in range(fx):
                ys[slot_of(s), j * fx + x : j * fx + x + 1, :] = target[i, x, y : y + 1, :]
        packed = jnp.zeros((fy, LANES), jnp.float32)
        for j, i in enumerate(FACE[2, s]):
            for x in range(fx):
                packed = jnp.where(lane == j * fx + x, target[i, x, :, z : z + 1], packed)
        zs[slot_of(s)] = packed
        for i in FACE[2, s]:
            c = VELOCITIES[i]
            if c[1]:
                y = side(c[1], fy)
                es[EDGES.index(i)] = packed[y : y + 1]


def finish(*refs):
    levels = (refs[0:5], refs[5:10])
    outs, targets, store_sem = refs[10:12], refs[12:14], refs[14]
    stores = []
    for n in (0, 1):
        target = targets[n]
        source, xr, yr, zr, er = levels[n]
        _, fx, fy, fz = target.shape
        lane = lax.broadcasted_iota(jnp.int32, (fy, LANES), 1)
        row = lax.broadcasted_iota(jnp.int32, (fy, LANES), 0)
        last = lax.broadcasted_iota(jnp.int32, (fy, fz), 1)
        columns = []
        for s in SIGNS:
            column = zr[slot_of(s)]
            for j, i in enumerate(FACE[2, s]):
                c = VELOCITIES[i]
                if c[0]:
                    value = jnp.sum(
                        jnp.where(row == lane, er[EDGES.index(i)], 0.0), axis=1, keepdims=True
                    )
                    column = jnp.where(lane == j * fx + side(c[0], fx), value, column)
                elif c[1]:
                    spot = (lane >= j * fx) & (lane < (j + 1) * fx) & (row == side(c[1], fy))
                    column = jnp.where(spot, er[EDGES.index(i)], column)
            columns.append(column)
        for i in range(19):
            c = VELOCITIES[i]
            target[i] = source[i]
            if c[0]:
                target[i, side(c[0], fx)] = xr[slot_of(c[0]), FACE[0, c[0]].index(i)]
            if c[1]:
                y, j = side(c[1], fy), FACE[1, c[1]].index(i)
                for x in range(fx):
                    if c[0] and x == side(c[0], fx):
                        piece = er[EDGES.index(i), :, 0:fz]
                    else:
                        piece = yr[slot_of(c[1]), j * fx + x : j * fx + x + 1, :]
                    target[i, x, y : y + 1, :] = piece
            if c[2]:
                j, column = FACE[2, c[2]].index(i), columns[slot_of(c[2])]
                for x in range(fx):
                    k = j * fx + x
                    target[i, x] = jnp.where(
                        last == side(c[2], fz), column[:, k : k + 1], target[i, x]
                    )
            store = pltpu.make_async_copy(target.at[i], outs[n].at[i], store_sem.at[n, i])
            store.start()
            stores.append(store)
    for store in stores:
        store.wait()


def kernel(
    sizes, slots, pop_in, cpop_in, fmask_in, cmask_in, bead_in, bins_in,
    stream, fxr, fyr, fzr, fer, cstream, cxr, cyr, czr, cer,
    pops, cpops, fmask, cmask, bead_ref, bins_ref, summed, restricted, parent, wide, tall, force,
    bead_send, bead_recv, bead_tiles, fxs, fys, fzs, fes, cxs, cys, czs, ces,
    in_sem, bead_sem, send_sem, recv_sem,
):
    ngx, ngy, ngz = sizes
    gx, gy, gz = lax.axis_index("gx"), lax.axis_index("gy"), lax.axis_index("gz")
    owners = ngx * ngy
    me = gx * ngy + gy
    _, nx, ny, nz = pops.shape
    _, hx, hy, hz = cpops.shape
    chunks = bins_ref.shape[0]
    per = LANES // slots

    loads = [
        pltpu.make_async_copy(src, dst, in_sem.at[n])
        for n, (src, dst) in enumerate(
            (
                (bead_in, bead_ref), (bins_in, bins_ref),
                (pop_in, pops), (cpop_in, cpops), (fmask_in, fmask), (cmask_in, cmask),
            )
        )
    ]
    for load in loads:
        load.start()

    def device(offset):
        return (
            lax.rem(gx + (offset[0] + ngx), ngx),
            lax.rem(gy + (offset[1] + ngy), ngy),
            lax.rem(gz + (offset[2] + ngz), ngz),
        )

    def owner(step):
        other = lax.rem(me + step, owners)
        return other, (other // ngy, lax.rem(other, ngy), gz)

    def each_peer(act):
        if owners > 32:
            pl.loop(1, owners)(act)
        else:
            for step in sorted(range(1, owners), key=lambda n: -min(n, owners - n)):
                act(step)

    barrier = pltpu.get_barrier_semaphore()
    cross = [(0, 0, 1), (0, 0, -1)] + [VELOCITIES[i] for i in EDGES if VELOCITIES[i][2]]
    @each_peer
    def _(step):
        pl.semaphore_signal(barrier, inc=1, device_id=owner(step)[1], device_id_type=MESH)

    for offset in cross:
        pl.semaphore_signal(barrier, inc=1, device_id=device(offset), device_id_type=MESH)

    for load in loads[:2]:
        load.wait()
    for chunk in range(chunks):
        bead_send[chunk, 0:6, :] = bead_ref[pl.ds(chunk, 6, stride=chunks), :]
        bead_send[chunk, 6:7, :] = bins_ref[chunk : chunk + 1, :].astype(jnp.float32)
        bead_send[chunk, 7:8, :] = jnp.zeros((1, LANES), jnp.float32)
    bead_recv[me] = bead_send[me // per]

    pl.semaphore_wait(barrier, len(cross) + owners - 1)

    @each_peer
    def _(step):
        other, where = owner(step)
        pltpu.make_async_remote_copy(
            src_ref=bead_send.at[other // per],
            dst_ref=bead_recv.at[me],
            send_sem=bead_sem.at[0],
            recv_sem=bead_sem.at[1],
            device_id=where,
            device_id_type=MESH,
        ).start()

    for load in loads[2:]:
        load.wait()

    @pl.loop(0, 19)
    def _(q):
        for x in range(hx):
            total = None
            for i in range(2):
                for j in range(2):
                    piece = pops[q, 2 * x + i, pl.ds(j, hy, stride=2), :]
                    total = piece if total is None else total + piece
            summed[q, x] = total

    fold = lax.broadcasted_iota(jnp.int32, (nz, hz), 0) - 2 * lax.broadcasted_iota(
        jnp.int32, (nz, hz), 1
    )
    fold = jnp.where((fold == 0) | (fold == 1), 0.125, 0.0).astype(jnp.bfloat16)
    restricted[...] = times_exact(summed[...].reshape(19 * hx * hy, nz), fold).reshape(
        19, hx, hy, hz
    )

    @pl.loop(0, hx)
    def _(x):
        p = [restricted[i, x] for i in range(19)]
        rho, m = moments(p)
        inv = 1.0 / rho
        pre = relax(p, rho, [v * inv for v in m], TO_COARSE, 1.0 - TO_COARSE)
        live = cmask[x] == 1
        pre = [jnp.where(live, pre[i], cpops[i, x]) for i in range(19)]
        rho, m = moments(pre)
        inv = 1.0 / rho
        u = [v * inv for v in m]
        down = relax(pre, rho, u, TO_FINE, 1.0 - TO_FINE)
        post = relax(pre, rho, u, 1.0 - 1.0 / TAU_COARSE, 1.0 / TAU_COARSE)
        for i in range(19):
            c = VELOCITIES[i]
            parent[i, x] = down[i]
            cstream[i, lax.rem(x + (c[0] + hx), hx)] = moved(post[i], c)

    spread = lax.broadcasted_iota(jnp.int32, (hz, nz), 1) - 2 * lax.broadcasted_iota(
        jnp.int32, (hz, nz), 0
    )
    spread = jnp.where((spread == 0) | (spread == 1), 1.0, 0.0).astype(jnp.bfloat16)
    wide[...] = times_exact(parent[...].reshape(19 * hx * hy, hz), spread).reshape(19, hx, hy, nz)

    @pl.loop(0, 19)
    def _(q):
        for x in range(hx):
            value = wide[q, x]
            tall[x, pl.ds(0, hy, stride=2), :] = value
            tall[x, pl.ds(1, hy, stride=2), :] = value
        for x in range(nx):
            pops[q, x] = jnp.where(fmask[x] == 1, pops[q, x], tall[x // 2])

    copies = []

    def send(src, dst, offset):
        n = len(copies)
        copy = pltpu.make_async_remote_copy(
            src_ref=src, dst_ref=dst, send_sem=send_sem.at[n], recv_sem=recv_sem.at[n],
            device_id=device(offset), device_id_type=MESH,
        )
        copy.start()
        copies.append(copy)

    def send_x(xs, xr, es, er):
        for s in SIGNS:
            send(xs.at[slot_of(s)], xr.at[slot_of(s)], (s, 0, 0))
        for n, i in enumerate(EDGES):
            if VELOCITIES[i][0]:
                send(es.at[n], er.at[n], VELOCITIES[i])

    def send_yz(ys, yr, zs, zr, es, er):
        for s in SIGNS:
            send(ys.at[slot_of(s)], yr.at[slot_of(s)], (0, s, 0))
            send(zs.at[slot_of(s)], zr.at[slot_of(s)], (0, 0, s))
        for n, i in enumerate(EDGES):
            if not VELOCITIES[i][0]:
                send(es.at[n], er.at[n], VELOCITIES[i])

    pack_x(cstream, cxs, ces)
    send_x(cxs, cxr, ces, cer)
    pack_yz(cstream, cys, czs, ces)
    send_yz(cys, cyr, czs, czr, ces, cer)

    arrived = bead_recv.at[pl.ds(0, owners - 1)]
    pltpu.make_async_copy(arrived, arrived, bead_sem.at[1]).wait()
    lane = lax.broadcasted_iota(jnp.int32, (8, LANES), 1)
    mine = lax.rem(me, per)

    @pl.loop(0, owners // per)
    def _(t):
        tile = jnp.zeros((8, LANES), jnp.float32)
        for k in range(per):
            turned = pltpu.roll(
                bead_recv[t * per + k], lax.rem((k + per - mine) * slots, LANES), 1
            )
            tile = jnp.where((lane >= k * slots) & (lane < (k + 1) * slots), turned, tile)
        bead_tiles[t] = tile

    bins_y, bins_z = ny // 2, nz // BIN_Z

    def window(start, position, live, cells, span):
        offset = lax.broadcasted_iota(jnp.int32, (cells, LANES), 0).astype(jnp.float32) - start
        distance = offset - position
        inside = (offset >= 0.0) & (offset < span) & live
        return jnp.where(inside, jnp.exp(-0.5 * distance * distance), 0.0)

    def operands(t):
        tile = bead_tiles[t]
        number = tile[6:7]
        live = number >= 0.0
        bx = jnp.floor((number + 0.5) * (1.0 / (bins_y * bins_z)))
        rest = number - bx * (bins_y * bins_z)
        by = jnp.floor((rest + 0.5) * (1.0 / bins_z))
        bz = rest - by * bins_z
        wx = window(2.0 * bx, tile[0:1], live, nx, 2.0)
        wy = window(2.0 * by, tile[1:2], live, ny, 2.0)
        wz = window(float(BIN_Z) * bz, tile[2:3], live, nz, float(BIN_Z))
        rows = []
        for d in range(3):
            pushed = wx * tile[3 + d : 4 + d]
            for x in range(nx):
                rows.append(pushed[x : x + 1] * wy)
        lh, ll = parts(jnp.concatenate(rows, axis=0))
        rh, rl = parts(wz)
        return [lh, lh, ll], [rh, rl, rh]

    tiles = owners // per
    group = next(n for n in (4, 2, 1) if tiles % n == 0)

    def add_force(g):
        left, right = [], []
        for n in range(group):
            more = operands(g * group + n)
            left += more[0]
            right += more[1]
        total = lax.dot_general(
            jnp.concatenate(left, axis=1),
            jnp.concatenate(right, axis=1),
            (((1,), (1,)), ((), ())),
            preferred_element_type=jnp.float32,
        ).reshape(3, nx, ny, nz)
        if tiles == group:
            force[...] = total
        else:
            force[...] += total

    if tiles == group:
        add_force(0)
    else:
        force[...] = jnp.zeros_like(force)
        pl.loop(0, tiles // group)(add_force)

    def collide(k):
        x = lax.rem(k + (nx - 1), nx)
        p = [pops[i, x] for i in range(19)]
        f = [force[d, x] for d in range(3)]
        rho, m = moments(p)
        inv = 1.0 / rho
        u = [(v + 0.5 * w) * inv for v, w in zip(m, f)]
        post = relax(
            p, rho, u, 1.0 - 1.0 / TAU_FINE, 1.0 / TAU_FINE, f, 1.0 - 0.5 / TAU_FINE
        )
        for i in range(19):
            c = VELOCITIES[i]
            stream[i, lax.rem(x + (c[0] + nx), nx)] = moved(post[i], c)

    pl.loop(0, 2)(collide)
    pack_x(stream, fxs, fes)
    send_x(fxs, fxr, fes, fer)
    pl.loop(2, nx)(collide)
    pack_yz(stream, fys, fzs, fes)
    send_yz(fys, fyr, fzs, fzr, fes, fer)
    pltpu.make_async_copy(arrived, arrived, bead_sem.at[0]).wait()
    for copy in copies:
        copy.wait()


def local(populations, coarse_pops, fine_mask, coarse_mask, bead_data, bead_bins):
    _, nx, ny, nz = populations.shape
    _, hx, hy, hz = coarse_pops.shape
    sizes = tuple(lax.axis_size(axis) for axis in ("gx", "gy", "gz"))
    owners = sizes[0] * sizes[1]
    total = bead_data.shape[4]
    chunks = total // LANES
    slots = total // owners
    beads = bead_data.reshape(6 * chunks, LANES)
    bins = bead_bins.reshape(chunks, LANES)
    f32, i32 = jnp.float32, jnp.int32
    any_spec = pl.BlockSpec(memory_space=pl.ANY)
    hbm_spec = pl.BlockSpec(memory_space=pltpu.HBM)
    vmem_spec = pl.BlockSpec(memory_space=pltpu.VMEM)
    dma = pltpu.SemaphoreType.DMA

    def rim(fx, fy, fz):
        return [(2, 5, fy, fz), (2, 5 * fx, fz), (2, fy, LANES), (12, 1, LANES)]

    fine_rim, coarse_rim = rim(nx, ny, nz), rim(hx, hy, hz)
    shapes = [populations.shape, *fine_rim, coarse_pops.shape, *coarse_rim]
    pieces = pl.pallas_call(
        functools.partial(kernel, sizes, slots),
        out_shape=[jax.ShapeDtypeStruct(shape, f32) for shape in shapes],
        in_specs=[hbm_spec] * 6,
        out_specs=([vmem_spec] + [any_spec] * 4) * 2,
        scratch_shapes=[
            pltpu.VMEM((19, nx, ny, nz), f32),
            pltpu.VMEM((19, hx, hy, hz), f32),
            pltpu.VMEM((nx, ny, nz), i32),
            pltpu.VMEM((hx, hy, hz), i32),
            pltpu.VMEM((6 * chunks, LANES), f32),
            pltpu.VMEM((chunks, LANES), i32),
            pltpu.VMEM((19, hx, hy, nz), f32),
            pltpu.VMEM((19, hx, hy, hz), f32),
            pltpu.VMEM((19, hx, hy, hz), f32),
            pltpu.VMEM((19, hx, hy, nz), f32),
            pltpu.VMEM((hx, ny, nz), f32),
            pltpu.VMEM((3, nx, ny, nz), f32),
            pltpu.VMEM((chunks, 8, LANES), f32),
            pltpu.VMEM((owners, 8, LANES), f32),
            pltpu.VMEM((total // LANES, 8, LANES), f32),
            *[pltpu.VMEM(shape, f32) for shape in fine_rim + coarse_rim],
            dma((6,)),
            dma((2,)),
            dma((36,)),
            dma((36,)),
        ],
        compiler_params=pltpu.CompilerParams(
            collective_id=0, has_side_effects=True, vmem_limit_bytes=LIMIT
        ),
    )(*[pltpu.with_memory_space_constraint(v, pltpu.HBM) for v in (populations, coarse_pops, fine_mask, coarse_mask, beads, bins)])
    return tuple(
        pl.pallas_call(
            finish,
            out_shape=[
                jax.ShapeDtypeStruct(populations.shape, f32),
                jax.ShapeDtypeStruct(coarse_pops.shape, f32),
            ],
            in_specs=[vmem_spec] * len(shapes),
            out_specs=[any_spec] * 2,
            scratch_shapes=[
                pltpu.VMEM(populations.shape, f32),
                pltpu.VMEM(coarse_pops.shape, f32),
                dma((2, 19)),
            ],
            compiler_params=pltpu.CompilerParams(vmem_limit_bytes=LIMIT),
        )(*pieces)
    )


def solution(mesh):
    in_specs = (
        P(None, "gx", "gy", "gz"),
        P(None, "gx", "gy", "gz"),
        P("gx", "gy", "gz"),
        P("gx", "gy", "gz"),
        P("gx", "gy", "gz", None, None),
        P("gx", "gy", "gz", None, None),
    )
    out_specs = (P(None, "gx", "gy", "gz"), P(None, "gx", "gy", "gz"))
    return jax.shard_map(local, mesh=mesh, in_specs=in_specs, out_specs=out_specs, check_vma=False)
```

profile of v0, /device:TPU:0, one launch (start us, length us, event | category | flops | bytes accessed | tf_op | source)
XLA Modules:
  0.0 21.1 jit_solution(17881189726209546536)
XLA Ops:
  0.6 18.9 %shard_map.77 = (f32[19,8,16,128]{3,2,1,0:T(8,128)S(1)}, f32[2,5,16,128]{3,2,1,0:T(8,128)S(1)}, f32[2,40,128]{2,1,0:T(8,128)S(1)}, f32[2,16,128]{2,1,0:T(8,128)S...) custom-call(f32[19,8,16,128]{3,2,1,0:T(8,128)} %pop_in.1, ...), custom_call_target="tpu_custom_call" | custom-call | tf_op jit(solution)/shard_map/pallas_call | solution.py:470
  19.6 1.6 %shard_map.78 = (f32[19,8,16,128]{3,2,1,0:T(8,128)}, f32[19,4,8,64]{3,2,1,0:T(8,128)}) custom-call(f32[19,8,16,128]{3,2,1,0:T(8,128)S(1)} %get-tuple-element.12.refs_0_, f32[2,5,16,128]{3,2,1,0:T(8,128)S(1)} %get-tuple-element.13.refs_1_, f32[2,40,128]{2,1,0:T(8,128)S(1)} %get-tuple-element.14.refs_2_, f32[2,16,128]{2,1,0:T(8,128)S(1)} %get-tuple-element.15.refs_3_, ...), custom_call_target="tpu_custom_call" | custom-call | tf_op jit(solution)/shard_map/pallas_call | solution.py:502
where the time goes:
time: 21.4 us; the launch traced here: 21.1 us
  Pallas kernels  20.5 us (96%)
  between operations  0.64 us (3%)
    pallas_call x1, Pallas kernels, local(): pl.pallas_call(functools.partial(kernel, sizes, slots), out_shape=[jax.Sh...  18.9 us
    pallas_call x1, Pallas kernels, local(): pl.pallas_call(finish, out_shape=[jax.ShapeDtypeStruct(populations.shape,...  1.57 us

commit v1 on v0

v1 whole, which is shorter than its diff:
```python
import functools

import jax
import jax.numpy as jnp
from jax import lax
from jax.experimental import pallas as pl
from jax.experimental.pallas import tpu as pltpu
from jax.sharding import PartitionSpec as P

BIN_Z = 32
VELOCITIES = [
    (0, 0, 0), (1, 0, 0), (-1, 0, 0), (0, 1, 0), (0, -1, 0), (0, 0, 1), (0, 0, -1),
    (1, 1, 0), (-1, -1, 0), (1, -1, 0), (-1, 1, 0), (1, 0, 1), (-1, 0, -1), (1, 0, -1),
    (-1, 0, 1), (0, 1, 1), (0, -1, -1), (0, 1, -1), (0, -1, 1),
]
WEIGHTS = [1.0 / 3.0] + [1.0 / 18.0] * 6 + [1.0 / 36.0] * 12
TAU_FINE = 1.2
TAU_COARSE = 0.85
TO_COARSE = 2.0 * TAU_COARSE / TAU_FINE
TO_FINE = TAU_FINE / (2.0 * TAU_COARSE)
LANES = 128
FIELDS = 8
LIMIT = 24 * 2**20
MESH = pl.DeviceIdType.MESH
SIGNS = (1, -1)
FACE = {(a, s): [i for i in range(19) if VELOCITIES[i][a] == s] for a in range(3) for s in SIGNS}
EDGES = [i for i in range(7, 19)]
EDGES_YZ = [i for i in EDGES if not VELOCITIES[i][0]]


def along(vector, c):
    total = None
    for part, sign in zip(vector, c):
        if sign:
            total = part if total is None else (total + part if sign > 0 else total - part)
    return total


def moments(p):
    rho = p[0]
    sums = [None] * 19
    m = [None] * 3
    for i in range(1, 19, 2):
        rho = rho + (p[i] + p[i + 1])
        sums[i] = p[i] - p[i + 1]
        for axis, sign in enumerate(VELOCITIES[i]):
            if sign:
                if m[axis] is None:
                    m[axis] = sums[i]
                else:
                    m[axis] = m[axis] + sums[i] if sign > 0 else m[axis] - sums[i]
    return rho, m


def relax(p, rho, u, a, b, force=None, k=0.0):
    scaled = b * rho
    base = scaled * (1.0 - 1.5 * (u[0] * u[0] + u[1] * u[1] + u[2] * u[2]))
    lin = [3.0 * scaled * v for v in u]
    quad = [4.5 * scaled * v for v in u]
    if force is not None:
        base = base - (3.0 * k) * (u[0] * force[0] + u[1] * force[1] + u[2] * force[2])
        lin = [v + (3.0 * k) * f for v, f in zip(lin, force)]
        quad = [v + (9.0 * k) * f for v, f in zip(quad, force)]
    out = [None] * 19
    if p[0] is not None:
        out[0] = a * p[0] + WEIGHTS[0] * base
    for i in range(1, 19, 2):
        if p[i] is None and p[i + 1] is None:
            continue
        c, w = VELOCITIES[i], WEIGHTS[i]
        even = w * (base + along(u, c) * along(quad, c))
        odd = w * along(lin, c)
        if p[i] is not None:
            out[i] = a * p[i] + (even + odd)
        if p[i + 1] is not None:
            out[i + 1] = a * p[i + 1] + (even - odd)
    return out


def parts(x):
    high = x.astype(jnp.bfloat16)
    return high, (x - high.astype(jnp.float32)).astype(jnp.bfloat16)


def times_exact(x, table):
    high, low = parts(x)
    dot = functools.partial(jnp.dot, preferred_element_type=jnp.float32)
    return dot(high, table) + dot(low, table)


def moved(plane, c):
    rows, lanes = plane.shape
    if c[1]:
        plane = pltpu.roll(plane, 1 if c[1] > 0 else rows - 1, 0)
    if c[2]:
        plane = pltpu.roll(plane, 1 if c[2] > 0 else lanes - 1, 1)
    return plane


def side(sign, length):
    return 0 if sign > 0 else length - 1


def slot_of(sign):
    return 0 if sign > 0 else 1


def pack_x(target, xs, es):
    _, fx, fy, fz = target.shape
    row = lax.broadcasted_iota(jnp.int32, (fy, LANES), 0)
    diagonal = row == lax.broadcasted_iota(jnp.int32, (fy, LANES), 1)
    for s in SIGNS:
        for j, i in enumerate(FACE[0, s]):
            plane = target[i, side(s, fx)]
            xs[slot_of(s), j] = plane
            c = VELOCITIES[i]
            if c[1]:
                y = side(c[1], fy)
                es[EDGES.index(i), :, 0:fz] = plane[y : y + 1]
            elif c[2]:
                z = side(c[2], fz)
                turned = jnp.where(diagonal, plane[:, z : z + 1], 0.0)
                es[EDGES.index(i)] = jnp.sum(turned, axis=0, keepdims=True)


def pack_yz(target, ys, zs, es):
    _, fx, fy, fz = target.shape
    lane = lax.broadcasted_iota(jnp.int32, (fy, LANES), 1)
    for s in SIGNS:
        y, z = side(s, fy), side(s, fz)
        for j, i in enumerate(FACE[1, s]):
            for x in range(fx):
                ys[slot_of(s), j * fx + x] = target[i, x, y : y + 1, :]
        packed = jnp.zeros((fy, LANES), jnp.float32)
        for j, i in enumerate(FACE[2, s]):
            for x in range(fx):
                packed = jnp.where(lane == j * fx + x, target[i, x, :, z : z + 1], packed)
        zs[slot_of(s)] = packed
        for i in FACE[2, s]:
            c = VELOCITIES[i]
            if c[1]:
                y = side(c[1], fy)
                es[EDGES.index(i)] = packed[y : y + 1]


def finish(*refs):
    levels = ((refs[0], None, *refs[1:4], EDGES_YZ), (*refs[4:9], EDGES))
    outs, targets, store_sem = refs[9:11], refs[11:13], refs[13]
    stores = []
    for n in (0, 1):
        target = targets[n]
        source, xr, yr, zr, er, edges = levels[n]
        _, fx, fy, fz = target.shape
        lane = lax.broadcasted_iota(jnp.int32, (fy, LANES), 1)
        row = lax.broadcasted_iota(jnp.int32, (fy, LANES), 0)
        last = lax.broadcasted_iota(jnp.int32, (fy, fz), 1)
        columns = []
        for s in SIGNS:
            column = zr[slot_of(s)]
            for j, i in enumerate(FACE[2, s]):
                c = VELOCITIES[i]
                if c[0] and xr is not None:
                    value = jnp.sum(
                        jnp.where(row == lane, er[edges.index(i)], 0.0), axis=1, keepdims=True
                    )
                    column = jnp.where(lane == j * fx + side(c[0], fx), value, column)
                elif c[1]:
                    spot = (lane >= j * fx) & (lane < (j + 1) * fx) & (row == side(c[1], fy))
                    column = jnp.where(spot, er[edges.index(i)], column)
            columns.append(column)
        for i in range(19):
            c = VELOCITIES[i]
            target[i] = source[i]
            if c[0] and xr is not None:
                target[i, side(c[0], fx)] = xr[slot_of(c[0]), FACE[0, c[0]].index(i)]
            if c[1]:
                y, j = side(c[1], fy), FACE[1, c[1]].index(i)
                for x in range(fx):
                    if c[0] and xr is not None and x == side(c[0], fx):
                        piece = er[edges.index(i), :, 0:fz]
                    else:
                        piece = yr[slot_of(c[1]), j * fx + x]
                    target[i, x, y : y + 1, :] = piece
            if c[2]:
                j, column = FACE[2, c[2]].index(i), columns[slot_of(c[2])]
                for x in range(fx):
                    k = j * fx + x
                    target[i, x] = jnp.where(
                        last == side(c[2], fz), column[:, k : k + 1], target[i, x]
                    )
            store = pltpu.make_async_copy(target.at[i], outs[n].at[i], store_sem.at[n, i])
            store.start()
            stores.append(store)
    for store in stores:
        store.wait()


def repeat(count, act, most=8):
    if count > most:
        pl.loop(0, count)(act)
    else:
        for n in range(count):
            act(n)


def kernel(
    sizes, slots, pop_in, cpop_in, fmask_in, cmask_in, bead_in, bins_in,
    stream, fyr, fzr, fer, cstream, cxr, cyr, czr, cer,
    pops, cpops, fmask, cmask, bead_ref, bins_ref, summed, restricted, parent, wide, tall,
    force, halo_force, totals, halo_send, halo_recv,
    bead_rows, bead_send, bead_recv, fys, fzs, fes, cxs, cys, czs, ces,
    in_sem, bead_sem, send_sem, recv_sem,
):
    ngx, ngy, ngz = sizes
    gx, gy, gz = lax.axis_index("gx"), lax.axis_index("gy"), lax.axis_index("gz")
    owners = ngx * ngy
    me = gx * ngy + gy
    _, nx, ny, nz = pops.shape
    _, hx, hy, hz = cpops.shape
    chunks = bins_ref.shape[0]
    per = LANES // slots
    f32 = jnp.float32

    ends = [(0, 2), (nx - 2, 2)]
    middle = [(2, nx - 4)]
    loads = [
        pltpu.make_async_copy(src, dst, in_sem.at[n])
        for n, (src, dst) in enumerate(
            [(bead_in, bead_ref), (bins_in, bins_ref)]
            + [(pop_in.at[:, pl.ds(x, w)], pops.at[:, pl.ds(x, w)]) for x, w in ends]
            + [(cmask_in, cmask), (fmask_in, fmask), (cpop_in, cpops)]
            + [(pop_in.at[:, pl.ds(x, w)], pops.at[:, pl.ds(x, w)]) for x, w in middle]
        )
    ]
    for load in loads:
        load.start()

    def device(offset):
        return (
            lax.rem(gx + (offset[0] + ngx), ngx),
            lax.rem(gy + (offset[1] + ngy), ngy),
            lax.rem(gz + (offset[2] + ngz), ngz),
        )

    def owner(step):
        other = lax.rem(me + step, owners)
        return other, (other // ngy, lax.rem(other, ngy), gz)

    def each_peer(act):
        if owners > 32:
            pl.loop(1, owners)(act)
        else:
            for step in sorted(range(1, owners), key=lambda n: -min(n, owners - n)):
                act(step)

    barrier = pltpu.get_barrier_semaphore()
    cross = [(0, 0, 1), (0, 0, -1)] + [VELOCITIES[i] for i in EDGES if VELOCITIES[i][2]]

    with jax.named_scope("p_signals"):
        @each_peer
        def _(step):
            pl.semaphore_signal(barrier, inc=1, device_id=owner(step)[1], device_id_type=MESH)

        for offset in cross:
            pl.semaphore_signal(barrier, inc=1, device_id=device(offset), device_id_type=MESH)

    lane = lax.broadcasted_iota(jnp.int32, (FIELDS, LANES), 1)
    sub = lax.broadcasted_iota(jnp.int32, (FIELDS, LANES), 0)
    diagonal = (lax.div(lane, slots) + (FIELDS - sub)) & (per - 1)
    turn = sub & (per - 1)

    def put_block(o, block):
        a, b = o // ngy, lax.rem(o, ngy)
        bead_send[b, a + 1] = block

    def pack_chunk(chunk):
        bead_rows[0:6, :] = bead_ref[pl.ds(chunk, 6, stride=chunks), :]
        bead_rows[6:7, :] = bins_ref[pl.ds(chunk, 1), :].astype(f32)
        rows = bead_rows[...]
        turned = rows
        for m in range(1, per):
            turned = jnp.where(turn == m, pltpu.roll(rows, slots * m, 1), turned)
        for k in range(per):
            kept = jnp.where(diagonal == k, turned, 0.0)
            shift = 1
            while shift < per:
                kept = kept + pltpu.roll(kept, FIELDS - shift, 0)
                shift *= 2
            block = [kept[n : n + 1] for n in range(0, FIELDS, per)]
            o = chunk * per + k
            a, b = (o // ngy, o % ngy) if isinstance(o, int) else (lax.div(o, ngy), lax.rem(o, ngy))
            for n, part in enumerate(block):
                bead_send[b, a + 1, pl.ds(n, 1), :] = part

    with jax.named_scope("p_pack"):
        for load in loads[:2]:
            load.wait()
        bead_rows[7:8, :] = jnp.zeros((1, LANES), f32)
        repeat(chunks, pack_chunk)
        for b in range(ngy):
            bead_send[b, 0] = bead_send[b, ngx]
            bead_send[b, ngx + 1] = bead_send[b, 1]
        bead_recv[me] = bead_send[gy, pl.ds(gx, 3)]

    def send_beads():
        pl.semaphore_wait(barrier, len(cross) + owners - 1)

        @each_peer
        def _(step):
            _, where = owner(step)
            pltpu.make_async_remote_copy(
                src_ref=bead_send.at[where[1], pl.ds(where[0], 3)],
                dst_ref=bead_recv.at[me],
                send_sem=bead_sem.at[0],
                recv_sem=bead_sem.at[1],
                device_id=where,
                device_id_type=MESH,
            ).start()

    early = gx * 3 < ngx

    with jax.named_scope("p_barrier"):
        @pl.when(jnp.logical_not(early))
        def _():
            send_beads()

    fold = lax.broadcasted_iota(jnp.int32, (nz, hz), 0) - 2 * lax.broadcasted_iota(
        jnp.int32, (nz, hz), 1
    )
    fold = jnp.where((fold == 0) | (fold == 1), 0.125, 0.0).astype(jnp.bfloat16)
    spread = lax.broadcasted_iota(jnp.int32, (hz, nz), 1) - 2 * lax.broadcasted_iota(
        jnp.int32, (hz, nz), 0
    )
    spread = jnp.where((spread == 0) | (spread == 1), 1.0, 0.0).astype(jnp.bfloat16)

    def prepare(start, count, step):
        @pl.loop(0, 19)
        def _(q):
            for n in range(count):
                total = None
                for i in range(2):
                    for j in range(2):
                        piece = pops[q, 2 * (start + n * step) + i, pl.ds(j, hy, stride=2), :]
                        total = piece if total is None else total + piece
                summed[n, q] = total

        rows = count * 19 * hy
        restricted[0:count] = times_exact(summed[0:count].reshape(rows, nz), fold).reshape(
            count, 19, hy, hz
        )

        @pl.loop(0, count)
        def _(n):
            x = start + n * step
            p = [restricted[n, i] for i in range(19)]
            rho, m = moments(p)
            inv = 1.0 / rho
            pre = relax(p, rho, [v * inv for v in m], TO_COARSE, 1.0 - TO_COARSE)
            live = cmask[x] == 1
            pre = [jnp.where(live, pre[i], cpops[i, x]) for i in range(19)]
            rho, m = moments(pre)
            inv = 1.0 / rho
            u = [v * inv for v in m]
            down = relax(pre, rho, u, TO_FINE, 1.0 - TO_FINE)
            post = relax(pre, rho, u, 1.0 - 1.0 / TAU_COARSE, 1.0 / TAU_COARSE)
            for i in range(19):
                c = VELOCITIES[i]
                parent[n, i] = down[i]
                cstream[i, lax.rem(x + (c[0] + hx), hx)] = moved(post[i], c)

        wide[0:count] = times_exact(parent[0:count].reshape(rows, hz), spread).reshape(
            count, 19, hy, nz
        )

        @pl.loop(0, 19)
        def _(q):
            for n in range(count):
                value = wide[n, q]
                tall[n, pl.ds(0, hy, stride=2), :] = value
                tall[n, pl.ds(1, hy, stride=2), :] = value
            for n in range(count):
                for i in range(2):
                    x = 2 * (start + n * step) + i
                    pops[q, x] = jnp.where(fmask[x] == 1, pops[q, x], tall[n])

    with jax.named_scope("p_ends"):
        for load in loads[2:7]:
            load.wait()
        prepare(0, 2, hx - 1)
        for s in SIGNS:
            x = nx - 1 if s > 0 else 0
            p = [pops[i, x] for i in range(19)]
            rho, m = moments(p)
            for n, value in enumerate([rho, *m, *[p[i] for i in FACE[0, s]]]):
                halo_send[slot_of(s), n] = value

    with jax.named_scope("p_barrier2"):
        @pl.when(early)
        def _():
            send_beads()

    copies = []

    def send(src, dst, offset):
        n = len(copies)
        copy = pltpu.make_async_remote_copy(
            src_ref=src, dst_ref=dst, send_sem=send_sem.at[n], recv_sem=recv_sem.at[n],
            device_id=device(offset), device_id_type=MESH,
        )
        copy.start()
        copies.append(copy)

    for s in SIGNS:
        send(halo_send.at[slot_of(s)], halo_recv.at[slot_of(s)], (s, 0, 0))

    with jax.named_scope("p_middle"):
        for load in loads[7:]:
            load.wait()
        prepare(1, hx - 2, 1)

    with jax.named_scope("p_csend"):
        pack_x(cstream, cxs, ces)
        for s in SIGNS:
            send(cxs.at[slot_of(s)], cxr.at[slot_of(s)], (s, 0, 0))
        pack_yz(cstream, cys, czs, ces)
        for s in SIGNS:
            send(cys.at[slot_of(s)], cyr.at[slot_of(s)], (0, s, 0))
            send(czs.at[slot_of(s)], czr.at[slot_of(s)], (0, 0, s))
        for n, i in enumerate(EDGES):
            send(ces.at[n], cer.at[n], VELOCITIES[i])
        for n in range(2):
            fzs[n] = jnp.zeros((ny, LANES), f32)

    with jax.named_scope("p_beadwait"):
        arrived = bead_recv.at[pl.ds(0, owners - 1)]
        pltpu.make_async_copy(arrived, arrived, bead_sem.at[1]).wait()

    bins_y, bins_z = ny // 2, nz // BIN_Z
    bins_xy = (nx // 2) * bins_y
    near = jnp.where(sub < per, 0, 1)

    def gathered(t, side_of, mine):
        source = [
            [
                jnp.broadcast_to(bead_recv[t * per + j, side_of, pl.ds(n, 1), :], (FIELDS, LANES))
                for n in range(FIELDS // per)
            ]
            for j in range(per)
        ]
        both = []
        for rows in source:
            value = rows[0]
            for n in range(1, FIELDS // per):
                value = jnp.where(sub >= n * per, rows[n], value)
            both.append(value)
        where = (diagonal + (per - mine)) & (per - 1)
        tile = None
        for m in range(per):
            mixed = both[m % per]
            for f in range(1, per):
                mixed = jnp.where(turn == f, both[(f + m) % per], mixed)
            if m:
                mixed = pltpu.roll(mixed, slots * m, 1)
            tile = mixed if tile is None else jnp.where(where == m, mixed, tile)
        return tile

    row_i = lax.div(sub, 2).astype(f32)
    row_j = (sub & 1).astype(f32)
    depth = lax.broadcasted_iota(jnp.int32, (BIN_Z, LANES), 0).astype(f32)
    own_rows = lax.broadcasted_iota(jnp.int32, (bins_xy, LANES), 0).astype(f32)
    side_rows = lax.broadcasted_iota(jnp.int32, (bins_y, LANES), 0).astype(f32)
    bf16 = jnp.bfloat16

    def operands(t, side_of, mine):
        tile = gathered(t, side_of, mine)
        number = tile[6:7]
        column = jnp.floor((number + 0.5) * (1.0 / bins_z))
        layer = number - column * bins_z
        dx, dy = row_i - tile[0:1], row_j - tile[1:2]
        weight = jnp.exp(-0.5 * (dx * dx + dy * dy))
        if side_of == 1:
            mask, picks = own_rows == column, range(4)
        elif side_of == 0:
            mask, picks = side_rows + float(bins_xy - bins_y) == column, (2, 3)
        else:
            mask, picks = side_rows == column, (0, 1)
        highs, lows = [], []
        for d in range(3):
            pushed = weight * tile[3 + d : 4 + d]
            high = pushed.astype(bf16).astype(f32)
            low = pushed - high
            for n in picks:
                highs.append(jnp.where(mask, high[n : n + 1], 0.0))
                lows.append(jnp.where(mask, low[n : n + 1], 0.0))
        lh = jnp.concatenate(highs, axis=0).astype(bf16)
        ll = jnp.concatenate(lows, axis=0).astype(bf16)
        dz = depth - tile[2:3]
        fall = jnp.exp(-0.5 * (dz * dz))
        fh = fall.astype(bf16).astype(f32)
        fl = fall - fh
        rh = jnp.concatenate([jnp.where(layer == n, fh, 0.0) for n in range(bins_z)], axis=0)
        rl = jnp.concatenate([jnp.where(layer == n, fl, 0.0) for n in range(bins_z)], axis=0)
        rh, rl = rh.astype(bf16), rl.astype(bf16)
        return [lh, lh, ll], [rh, rl, rh]

    tiles = owners // per
    group = next(n for n in (4, 2, 1) if tiles % n == 0)

    def product(g, side_of):
        mine = lax.rem(lax.rem(gx + (side_of - 1 + ngx), ngx) * ngy + gy, per)
        left, right = [], []
        for n in range(group):
            more = operands(g * group + n, side_of, mine)
            left += more[0]
            right += more[1]
        return lax.dot_general(
            jnp.concatenate(left, axis=1),
            jnp.concatenate(right, axis=1),
            (((1,), (1,)), ((), ())),
            preferred_element_type=f32,
        )

    def whole(side_of):
        if tiles == group:
            return product(0, side_of)
        rows = 12 * bins_xy if side_of == 1 else 6 * bins_y
        totals[0:rows] = jnp.zeros((rows, nz), f32)

        @pl.loop(0, tiles // group)
        def _(g):
            totals[0:rows] += product(g, side_of)

        return totals[0:rows]

    with jax.named_scope("p_force"):
        value = whole(1)
        for d in range(3):
            for i in range(2):
                for j in range(2):
                    for b in range(nx // 2):
                        start = ((d * 2 + i) * 2 + j) * bins_xy + b * bins_y
                        force[d, 2 * b + i, pl.ds(j, bins_y, stride=2), :] = value[
                            start : start + bins_y
                        ]

    with jax.named_scope("p_hforce"):
        for n, side_of in enumerate((0, 2)):
            value = whole(side_of)
            for d in range(3):
                for j in range(2):
                    start = (d * 2 + j) * bins_y
                    halo_force[n, d, pl.ds(j, bins_y, stride=2), :] = value[start : start + bins_y]

    wide_lane = lax.broadcasted_iota(jnp.int32, (ny, LANES), 1)

    def collide(p, rho, m, f, x):
        inv = 1.0 / rho
        u = [(v + 0.5 * w) * inv for v, w in zip(m, f)]
        post = relax(
            p, rho, u, 1.0 - 1.0 / TAU_FINE, 1.0 / TAU_FINE, f, 1.0 - 0.5 / TAU_FINE
        )
        columns = [fzs[n] for n in range(2)]
        for i in range(19):
            c = VELOCITIES[i]
            if post[i] is None:
                continue
            at = x + c[0]
            if isinstance(at, int) and not 0 <= at < nx:
                continue
            plane = moved(post[i], c)
            stream[i, at] = plane
            if c[1]:
                y = side(c[1], ny)
                fys[slot_of(c[1]), FACE[1, c[1]].index(i) * nx + at] = plane[y : y + 1]
            if c[2]:
                n, z = slot_of(c[2]), side(c[2], nz)
                k = FACE[2, c[2]].index(i) * nx + at
                columns[n] = jnp.where(wide_lane == k, plane[:, z : z + 1], columns[n])
        for n in range(2):
            fzs[n] = columns[n]

    def collide_own(x):
        p = [pops[i, x] for i in range(19)]
        rho, m = moments(p)
        collide(p, rho, m, [force[d, x] for d in range(3)], x)

    with jax.named_scope("p_collide"):
        collide_own(0)
        pl.loop(1, nx - 1)(collide_own)
        collide_own(nx - 1)

    with jax.named_scope("p_hwait"):
        for copy in copies[:2]:
            copy.wait_recv()

    with jax.named_scope("p_hcollide"):
        for s in SIGNS:
            n = slot_of(s)
            p = [None] * 19
            for j, i in enumerate(FACE[0, s]):
                p[i] = halo_recv[n, 4 + j]
            collide(
                p, halo_recv[n, 0], [halo_recv[n, 1 + d] for d in range(3)],
                [halo_force[n, d] for d in range(3)], -1 if s > 0 else nx,
            )

    with jax.named_scope("p_sendyz"):
        for s in SIGNS:
            send(fys.at[slot_of(s)], fyr.at[slot_of(s)], (0, s, 0))
        for n, i in enumerate(EDGES_YZ):
            y = side(VELOCITIES[i][1], ny)
            fes[n] = fzs[slot_of(VELOCITIES[i][2]), y : y + 1, :]
            send(fes.at[n], fer.at[n], VELOCITIES[i])
        for s in SIGNS:
            send(fzs.at[slot_of(s)], fzr.at[slot_of(s)], (0, 0, s))

    with jax.named_scope("p_final"):
        pltpu.make_async_copy(arrived, arrived, bead_sem.at[0]).wait()
        for copy in copies[:2]:
            copy.wait_send()
        for copy in copies[2:]:
            copy.wait()


def local(populations, coarse_pops, fine_mask, coarse_mask, bead_data, bead_bins):
    _, nx, ny, nz = populations.shape
    _, hx, hy, hz = coarse_pops.shape
    sizes = tuple(lax.axis_size(axis) for axis in ("gx", "gy", "gz"))
    owners = sizes[0] * sizes[1]
    total = bead_data.shape[4]
    chunks = total // LANES
    slots = total // owners
    per = LANES // slots
    rows = FIELDS // per
    beads = bead_data.reshape(6 * chunks, LANES)
    bins = bead_bins.reshape(chunks, LANES)
    f32, i32 = jnp.float32, jnp.int32
    any_spec = pl.BlockSpec(memory_space=pl.ANY)
    hbm_spec = pl.BlockSpec(memory_space=pltpu.HBM)
    vmem_spec = pl.BlockSpec(memory_space=pltpu.VMEM)
    dma = pltpu.SemaphoreType.DMA

    fine_rim = [(2, 5 * nx, 1, nz), (2, ny, LANES), (len(EDGES_YZ), 1, LANES)]
    coarse_rim = [(2, 5, hy, hz), (2, 5 * hx, 1, hz), (2, hy, LANES), (12, 1, LANES)]
    shapes = [populations.shape, *fine_rim, coarse_pops.shape, *coarse_rim]
    count = max(2, hx - 2)
    pieces = pl.pallas_call(
        functools.partial(kernel, sizes, slots),
        out_shape=[jax.ShapeDtypeStruct(shape, f32) for shape in shapes],
        in_specs=[hbm_spec] * 6,
        out_specs=[vmem_spec] + [any_spec] * 3 + [vmem_spec] + [any_spec] * 4,
        scratch_shapes=[
            pltpu.VMEM((19, nx, ny, nz), f32),
            pltpu.VMEM((19, hx, hy, hz), f32),
            pltpu.VMEM((nx, ny, nz), i32),
            pltpu.VMEM((hx, hy, hz), i32),
            pltpu.VMEM((6 * chunks, LANES), f32),
            pltpu.VMEM((chunks, LANES), i32),
            pltpu.VMEM((count, 19, hy, nz), f32),
            pltpu.VMEM((count, 19, hy, hz), f32),
            pltpu.VMEM((count, 19, hy, hz), f32),
            pltpu.VMEM((count, 19, hy, nz), f32),
            pltpu.VMEM((count, ny, nz), f32),
            pltpu.VMEM((3, nx, ny, nz), f32),
            pltpu.VMEM((2, 3, ny, nz), f32),
            pltpu.VMEM((12 * (nx // 2) * (ny // 2), nz), f32),
            pltpu.VMEM((2, 9, ny, nz), f32),
            pltpu.VMEM((2, 9, ny, nz), f32),
            pltpu.VMEM((FIELDS, LANES), f32),
            pltpu.VMEM((sizes[1], sizes[0] + 2, rows, LANES), f32),
            pltpu.VMEM((owners, 3, rows, LANES), f32),
            *[pltpu.VMEM(shape, f32) for shape in fine_rim + coarse_rim],
            dma((8,)),
            dma((2,)),
            dma((28,)),
            dma((28,)),
        ],
        compiler_params=pltpu.CompilerParams(
            collective_id=0, has_side_effects=True, vmem_limit_bytes=LIMIT
        ),
    )(*[pltpu.with_memory_space_constraint(v, pltpu.HBM) for v in (populations, coarse_pops, fine_mask, coarse_mask, beads, bins)])
    return tuple(
        pl.pallas_call(
            finish,
            out_shape=[
                jax.ShapeDtypeStruct(populations.shape, f32),
                jax.ShapeDtypeStruct(coarse_pops.shape, f32),
            ],
            in_specs=[vmem_spec] * len(shapes),
            out_specs=[any_spec] * 2,
            scratch_shapes=[
                pltpu.VMEM(populations.shape, f32),
                pltpu.VMEM(coarse_pops.shape, f32),
                dma((2, 19)),
            ],
            compiler_params=pltpu.CompilerParams(vmem_limit_bytes=LIMIT),
        )(*pieces)
    )


def solution(mesh):
    in_specs = (
        P(None, "gx", "gy", "gz"),
        P(None, "gx", "gy", "gz"),
        P("gx", "gy", "gz"),
        P("gx", "gy", "gz"),
        P("gx", "gy", "gz", None, None),
        P("gx", "gy", "gz", None, None),
    )
    out_specs = (P(None, "gx", "gy", "gz"), P(None, "gx", "gy", "gz"))
    return jax.shard_map(local, mesh=mesh, in_specs=in_specs, out_specs=out_specs, check_vma=False)
```

time: 21.4 us -> 18.7 us (0.87)
  Pallas kernels: 20.5 us -> 17.8 us
    pallas_call x1, Pallas kernels: 18.9 us -> 16.3 us  [local(): pl.pallas_call(functools.partial(kernel, sizes, slots), out_shape=[jax.Sh...]
where the time goes in v1:
time: 18.7 us; the launch traced here: 18.4 us
  Pallas kernels  17.8 us (95%)
  between operations  0.64 us (3%)
    pallas_call x1, Pallas kernels, local(): pl.pallas_call(functools.partial(kernel, sizes, slots), out_shape=[jax.Sh...  16.3 us
    pallas_call x1, Pallas kernels, local(): pl.pallas_call(finish, out_shape=[jax.ShapeDtypeStruct(populations.shape,...  1.47 us

profile of v1, /device:TPU:0, one launch (start us, length us, event | category | flops | bytes accessed | tf_op | source)
XLA Modules:
  0.0 18.4 jit_solution(7920792131342594730)
XLA Ops:
  0.6 16.3 %shard_map.77 = (f32[19,8,16,128]{3,2,1,0:T(8,128)S(1)}, f32[2,40,1,128]{3,2,1,0:T(1,128)S(1)}, f32[2,16,128]{2,1,0:T(8,128)S(1)}, f32[4,1,128]{2,1,0:T(1,128)S(...) custom-call(f32[19,8,16,128]{3,2,1,0:T(8,128)} %pop_in.1, ...), custom_call_target="tpu_custom_call" | custom-call | tf_op jit(solution)/shard_map/pallas_call | solution.py:647
  17.0 1.5 %shard_map.78 = (f32[19,8,16,128]{3,2,1,0:T(8,128)}, f32[19,4,8,64]{3,2,1,0:T(8,128)}) custom-call(f32[19,8,16,128]{3,2,1,0:T(8,128)S(1)} %get-tuple-element.11.refs_0_, f32[2,40,1,128]{3,2,1,0:T(1,128)S(1)} %get-tuple-element.12.refs_1_, f32[2,16,128]{2,1,0:T(8,128)S(1)} %get-tuple-element.13.refs_2_, f32[4,1,128]{2,1,0:T(1,128)S(1)} %get-tuple-element.14.refs_3_, ...), custom_call_target="tpu_custom_call" | custom-call | tf_op jit(solution)/shard_map/pallas_call | solution.py:683

commit v2 on v1

v2 whole, which is shorter than its diff:
```python
import functools

import jax
import jax.numpy as jnp
from jax import lax
from jax.experimental import pallas as pl
from jax.experimental.pallas import tpu as pltpu
from jax.sharding import PartitionSpec as P

BIN_Z = 32
VELOCITIES = [
    (0, 0, 0), (1, 0, 0), (-1, 0, 0), (0, 1, 0), (0, -1, 0), (0, 0, 1), (0, 0, -1),
    (1, 1, 0), (-1, -1, 0), (1, -1, 0), (-1, 1, 0), (1, 0, 1), (-1, 0, -1), (1, 0, -1),
    (-1, 0, 1), (0, 1, 1), (0, -1, -1), (0, 1, -1), (0, -1, 1),
]
WEIGHTS = [1.0 / 3.0] + [1.0 / 18.0] * 6 + [1.0 / 36.0] * 12
TAU_FINE = 1.2
TAU_COARSE = 0.85
TO_COARSE = 2.0 * TAU_COARSE / TAU_FINE
TO_FINE = TAU_FINE / (2.0 * TAU_COARSE)
LANES = 128
FIELDS = 8
LIMIT = 24 * 2**20
MESH = pl.DeviceIdType.MESH
SIGNS = (1, -1)
FACE = {(a, s): [i for i in range(19) if VELOCITIES[i][a] == s] for a in range(3) for s in SIGNS}
EDGES = [i for i in range(7, 19)]
EDGES_YZ = [i for i in EDGES if not VELOCITIES[i][0]]


def along(vector, c):
    total = None
    for part, sign in zip(vector, c):
        if sign:
            total = part if total is None else (total + part if sign > 0 else total - part)
    return total


def moments(p):
    rho = p[0]
    sums = [None] * 19
    m = [None] * 3
    for i in range(1, 19, 2):
        rho = rho + (p[i] + p[i + 1])
        sums[i] = p[i] - p[i + 1]
        for axis, sign in enumerate(VELOCITIES[i]):
            if sign:
                if m[axis] is None:
                    m[axis] = sums[i]
                else:
                    m[axis] = m[axis] + sums[i] if sign > 0 else m[axis] - sums[i]
    return rho, m


def setup(rho, u, b, force=None, k=0.0):
    scaled = b * rho
    base = scaled * (1.0 - 1.5 * (u[0] * u[0] + u[1] * u[1] + u[2] * u[2]))
    lin = [3.0 * scaled * v for v in u]
    quad = [4.5 * scaled * v for v in u]
    if force is not None:
        base = base - (3.0 * k) * (u[0] * force[0] + u[1] * force[1] + u[2] * force[2])
        lin = [v + (3.0 * k) * f for v, f in zip(lin, force)]
        quad = [v + (9.0 * k) * f for v, f in zip(quad, force)]
    return u, base, lin, quad


def halves(i, made):
    u, base, lin, quad = made
    first = i if i % 2 else i - 1
    c, w = VELOCITIES[first], WEIGHTS[first]
    odd = w * along(lin, c)
    return w * (base + along(u, c) * along(quad, c)), odd if i % 2 else -odd


def relax(p, rho, u, a, b, force=None, k=0.0):
    made = setup(rho, u, b, force, k)
    out = [None] * 19
    if p[0] is not None:
        out[0] = a * p[0] + WEIGHTS[0] * made[1]
    for i in range(1, 19, 2):
        if p[i] is None and p[i + 1] is None:
            continue
        even, odd = halves(i, made)
        if p[i] is not None:
            out[i] = a * p[i] + (even + odd)
        if p[i + 1] is not None:
            out[i + 1] = a * p[i + 1] + (even - odd)
    return out


def parts(x):
    high = x.astype(jnp.bfloat16)
    return high, (x - high.astype(jnp.float32)).astype(jnp.bfloat16)


def times_exact(x, table):
    high, low = parts(x)
    dot = functools.partial(jnp.dot, preferred_element_type=jnp.float32)
    return dot(high, table) + dot(low, table)


def moved(plane, c):
    rows, lanes = plane.shape
    if c[1]:
        plane = pltpu.roll(plane, 1 if c[1] > 0 else rows - 1, 0)
    if c[2]:
        plane = pltpu.roll(plane, 1 if c[2] > 0 else lanes - 1, 1)
    return plane


def side(sign, length):
    return 0 if sign > 0 else length - 1


def slot_of(sign):
    return 0 if sign > 0 else 1


def pack_x(target, xs, es):
    _, fx, fy, fz = target.shape
    row = lax.broadcasted_iota(jnp.int32, (fy, LANES), 0)
    diagonal = row == lax.broadcasted_iota(jnp.int32, (fy, LANES), 1)
    for s in SIGNS:
        for j, i in enumerate(FACE[0, s]):
            plane = target[i, side(s, fx)]
            xs[slot_of(s), j] = plane
            c = VELOCITIES[i]
            if c[1]:
                y = side(c[1], fy)
                es[EDGES.index(i), :, 0:fz] = plane[y : y + 1]
            elif c[2]:
                z = side(c[2], fz)
                turned = jnp.where(diagonal, plane[:, z : z + 1], 0.0)
                es[EDGES.index(i)] = jnp.sum(turned, axis=0, keepdims=True)


def pack_yz(target, ys, zs, es):
    _, fx, fy, fz = target.shape
    lane = lax.broadcasted_iota(jnp.int32, (fy, LANES), 1)
    for s in SIGNS:
        y, z = side(s, fy), side(s, fz)
        for j, i in enumerate(FACE[1, s]):
            for x in range(fx):
                ys[slot_of(s), j * fx + x] = target[i, x, y : y + 1, :]
        packed = jnp.zeros((fy, LANES), jnp.float32)
        for j, i in enumerate(FACE[2, s]):
            for x in range(fx):
                packed = jnp.where(lane == j * fx + x, target[i, x, :, z : z + 1], packed)
        zs[slot_of(s)] = packed
        for i in FACE[2, s]:
            c = VELOCITIES[i]
            if c[1]:
                y = side(c[1], fy)
                es[EDGES.index(i)] = packed[y : y + 1]


def fill_coarse(target, xr, yr, zr, er):
    _, fx, fy, fz = target.shape
    lane = lax.broadcasted_iota(jnp.int32, (fy, LANES), 1)
    row = lax.broadcasted_iota(jnp.int32, (fy, LANES), 0)
    last = lax.broadcasted_iota(jnp.int32, (fy, fz), 1)
    columns = []
    for s in SIGNS:
        column = zr[slot_of(s)]
        for j, i in enumerate(FACE[2, s]):
            c = VELOCITIES[i]
            if c[0]:
                value = jnp.sum(
                    jnp.where(row == lane, er[EDGES.index(i)], 0.0), axis=1, keepdims=True
                )
                column = jnp.where(lane == j * fx + side(c[0], fx), value, column)
            elif c[1]:
                spot = (lane >= j * fx) & (lane < (j + 1) * fx) & (row == side(c[1], fy))
                column = jnp.where(spot, er[EDGES.index(i)], column)
        columns.append(column)
    for i in range(1, 19):
        c = VELOCITIES[i]
        if c[0]:
            target[i, side(c[0], fx)] = xr[slot_of(c[0]), FACE[0, c[0]].index(i)]
        if c[1]:
            y, j = side(c[1], fy), FACE[1, c[1]].index(i)
            for x in range(fx):
                if c[0] and x == side(c[0], fx):
                    piece = er[EDGES.index(i), :, 0:fz]
                else:
                    piece = yr[slot_of(c[1]), j * fx + x]
                target[i, x, y : y + 1, :] = piece
        if c[2]:
            j, column = FACE[2, c[2]].index(i), columns[slot_of(c[2])]
            for x in range(fx):
                k = j * fx + x
                target[i, x] = jnp.where(
                    last == side(c[2], fz), column[:, k : k + 1], target[i, x]
                )


def finish(nx, fine, columns, coarse, fine_out, coarse_out, target, store_sem):
    _, height, nz = fine.shape
    ny = height // nx
    order = [i for i in range(19) if not VELOCITIES[i][2]]
    turned = [i for i in range(19) if VELOCITIES[i][2]]
    stores = [pltpu.make_async_copy(coarse, coarse_out, store_sem.at[19])]
    for i in order + turned:
        source = target.at[turned.index(i)] if i in turned else fine.at[i]
        stores.append(pltpu.make_async_copy(source, fine_out.at[i], store_sem.at[i]))
    for store in stores[: 1 + len(order)]:
        store.start()
    last = lax.broadcasted_iota(jnp.int32, (ny, nz), 1)
    row = lax.broadcasted_iota(jnp.int32, (ny, nz), 0)
    for n, i in enumerate(turned):
        c = VELOCITIES[i]
        column = columns[slot_of(c[2])]
        spot = last == side(c[2], nz)
        if c[1]:
            spot = spot & (row != side(c[1], ny))
        for x in range(nx):
            k = FACE[2, c[2]].index(i) * nx + x
            target[n, x * ny : (x + 1) * ny, :] = jnp.where(
                spot, column[:, k : k + 1], fine[i, x * ny : (x + 1) * ny, :]
            )
        stores[1 + len(order) + n].start()
    for store in stores:
        store.wait()


def repeat(count, act, most=8):
    if count > most:
        pl.loop(0, count)(act)
    else:
        for n in range(count):
            act(n)


def kernel(
    sizes, slots, pop_in, cpop_in, fmask_in, cmask_in, bead_in, bins_in,
    stream, fzr, cstream,
    pops, cpops, fmask, cmask, bead_ref, bins_ref, tall,
    force, halo_force, halo_send, halo_recv, brim_send, brim_recv,
    bead_rows, bead_send, bead_recv, fys, fzs, cxs, cys, czs, ces,
    fyr, fer, cxr, cyr, czr, cer,
    in_sem, bead_sem, tile_sem, ready_sem, cross_sem, send_sem, recv_sem,
):
    ngx, ngy, ngz = sizes
    gx, gy, gz = lax.axis_index("gx"), lax.axis_index("gy"), lax.axis_index("gz")
    owners = ngx * ngy
    me = gx * ngy + gy
    nx, ny, nz = fmask.shape
    _, hx, hy, hz = cpops.shape
    chunks = bins_ref.shape[0]
    per = LANES // slots
    tiles = owners // per
    f32 = jnp.float32

    ends = [(0, 2), (nx - 2, 2)]
    middle = [(2, nx - 4)]
    loads = [
        pltpu.make_async_copy(src, dst, in_sem.at[n])
        for n, (src, dst) in enumerate(
            [(bead_in, bead_ref), (bins_in, bins_ref)]
            + [(pop_in.at[:, pl.ds(x * ny, w * ny)], pops.at[:, pl.ds(x * ny, w * ny)]) for x, w in ends]
            + [(cmask_in, cmask), (fmask_in, fmask), (cpop_in, cpops)]
            + [(pop_in.at[:, pl.ds(x * ny, w * ny)], pops.at[:, pl.ds(x * ny, w * ny)]) for x, w in middle]
        )
    ]
    for load in loads:
        load.start()

    def plane_at(x):
        return pl.ds(x * ny, ny)

    def rows_at(y):
        return pl.ds(y, nx, stride=ny)

    def device(offset):
        return (
            lax.rem(gx + (offset[0] + ngx), ngx),
            lax.rem(gy + (offset[1] + ngy), ngy),
            lax.rem(gz + (offset[2] + ngz), ngz),
        )

    def place(o):
        return lax.div(o, ngy), lax.rem(o, ngy), gz

    def number(where):
        return (where[0] * ngy + where[1]) * ngz + where[2]

    def cross_peers(act, later):
        mine = number((gx, gy, gz))
        for offset in cross:
            where = device(offset)
            other = number(where)

            @pl.when(other > mine if later else other < mine)
            def _():
                act(where)

    def loop(start, stop, act):
        lax.fori_loop(start, stop, lambda n, carry: (act(n), carry)[1], 0)

    barrier = pltpu.get_barrier_semaphore()
    cross = [(0, 0, 1), (0, 0, -1)] + [VELOCITIES[i] for i in EDGES if VELOCITIES[i][2]]
    lower = jnp.int32(0)
    for offset in cross:
        lower = lower + (number(device(offset)) < number((gx, gy, gz))).astype(jnp.int32)

    with jax.named_scope("p_signals"):
        loop(
            0, owners - 1 - me,
            lambda n: pl.semaphore_signal(
                barrier, inc=1, device_id=place(owners - 1 - n), device_id_type=MESH
            ),
        )

        @pl.when(me > 0)
        def _():
            pl.semaphore_signal(barrier, inc=1, device_id=place(0), device_id_type=MESH)

        cross_peers(
            lambda where: pl.semaphore_signal(
                barrier, inc=1, device_id=where, device_id_type=MESH
            ),
            later=True,
        )

    lane = lax.broadcasted_iota(jnp.int32, (FIELDS, LANES), 1)
    sub = lax.broadcasted_iota(jnp.int32, (FIELDS, LANES), 0)
    diagonal = (lax.div(lane, slots) + (FIELDS - sub)) & (per - 1)
    turn = sub & (per - 1)

    def put_block(o, block):
        a, b = o // ngy, lax.rem(o, ngy)
        bead_send[b, a + 1] = block

    def pack_chunk(chunk):
        bead_rows[0:6, :] = bead_ref[pl.ds(chunk, 6, stride=chunks), :]
        bead_rows[6:7, :] = bins_ref[pl.ds(chunk, 1), :].astype(f32)
        rows = bead_rows[...]
        turned = rows
        for m in range(1, per):
            turned = jnp.where(turn == m, pltpu.roll(rows, slots * m, 1), turned)
        for k in range(per):
            kept = jnp.where(diagonal == k, turned, 0.0)
            shift = 1
            while shift < per:
                kept = kept + pltpu.roll(kept, FIELDS - shift, 0)
                shift *= 2
            block = [kept[n : n + 1] for n in range(0, FIELDS, per)]
            o = chunk * per + k
            a, b = (o // ngy, o % ngy) if isinstance(o, int) else (lax.div(o, ngy), lax.rem(o, ngy))
            for n, part in enumerate(block):
                bead_send[b, a + 1, pl.ds(n, 1), :] = part

    with jax.named_scope("p_barrier"):
        @pl.when(me > 0)
        def _():
            pl.semaphore_wait(barrier, me + lower)
            loop(
                1, me,
                lambda o: pl.semaphore_signal(
                    ready_sem.at[me // per], inc=1, device_id=place(o), device_id_type=MESH
                ),
            )

    with jax.named_scope("p_pack"):
        for load in loads[:2]:
            load.wait()
        bead_rows[7:8, :] = jnp.zeros((1, LANES), f32)
        repeat(chunks, pack_chunk)
        for b in range(ngy):
            bead_send[b, 0] = bead_send[b, ngx]
            bead_send[b, ngx + 1] = bead_send[b, 1]
        own_beads = pltpu.make_async_copy(
            bead_send.at[gy, pl.ds(gx, 3)], bead_recv.at[me], tile_sem.at[me // per]
        )
        own_beads.start()

    def send_beads(o):
        where = place(o)
        pltpu.make_async_remote_copy(
            src_ref=bead_send.at[where[1], pl.ds(where[0], 3)],
            dst_ref=bead_recv.at[me],
            send_sem=bead_sem,
            recv_sem=tile_sem.at[me // per],
            device_id=where,
            device_id_type=MESH,
        ).start()

    def reply_cross():
        cross_peers(
            lambda where: pl.semaphore_signal(
                cross_sem, inc=1, device_id=where, device_id_type=MESH
            ),
            later=False,
        )

    with jax.named_scope("p_answer"):
        @pl.when(me > 0)
        def _():
            loop(0, me, send_beads)
            reply_cross()

    fold = lax.broadcasted_iota(jnp.int32, (nz, hz), 0) - 2 * lax.broadcasted_iota(
        jnp.int32, (nz, hz), 1
    )
    fold = jnp.where((fold == 0) | (fold == 1), 0.125, 0.0).astype(jnp.bfloat16)
    spread = lax.broadcasted_iota(jnp.int32, (hz, nz), 1) - 2 * lax.broadcasted_iota(
        jnp.int32, (hz, nz), 0
    )
    spread = jnp.where((spread == 0) | (spread == 1), 1.0, 0.0).astype(jnp.bfloat16)

    def prepare(x):
        sums = []
        for q in range(19):
            total = None
            for i in range(2):
                for j in range(2):
                    piece = pops[q, pl.ds((2 * x + i) * ny + j, hy, stride=2), :]
                    total = piece if total is None else total + piece
            sums.append(total)
        restricted = times_exact(jnp.concatenate(sums, axis=0), fold)
        p = [restricted[i * hy : (i + 1) * hy] for i in range(19)]
        rho, m = moments(p)
        inv = 1.0 / rho
        pre = relax(p, rho, [v * inv for v in m], TO_COARSE, 1.0 - TO_COARSE)
        live = cmask[x] == 1
        pre = [jnp.where(live, pre[i], cpops[i, x]) for i in range(19)]
        rho, m = moments(pre)
        inv = 1.0 / rho
        u = [v * inv for v in m]
        down = relax(pre, rho, u, TO_FINE, 1.0 - TO_FINE)
        post = relax(pre, rho, u, 1.0 - 1.0 / TAU_COARSE, 1.0 / TAU_COARSE)
        for i in range(19):
            c = VELOCITIES[i]
            cstream[i, lax.rem(x + (c[0] + hx), hx)] = moved(post[i], c)
        wide = times_exact(jnp.concatenate(down, axis=0), spread)
        for q in range(19):
            value = wide[q * hy : (q + 1) * hy]
            tall[q, pl.ds(0, hy, stride=2), :] = value
            tall[q, pl.ds(1, hy, stride=2), :] = value
        for i in range(2):
            kept = fmask[2 * x + i] == 1
            at = plane_at(2 * x + i)
            for q in range(19):
                pops[q, at] = jnp.where(kept, pops[q, at], tall[q])

    with jax.named_scope("p_ends"):
        for load in loads[2:7]:
            load.wait()
        pl.loop(0, 2)(lambda n: prepare(n * (hx - 1)))
        for s in SIGNS:
            x = nx - 1 if s > 0 else 0
            p = [pops[i, plane_at(x)] for i in range(19)]
            rho, m = moments(p)
            for n, value in enumerate([rho, *m, *[p[i] for i in FACE[0, s]]]):
                halo_send[slot_of(s), n] = value
            for t in SIGNS:
                y = ny - 1 if t > 0 else 0
                for n, value in enumerate([rho, *m, p[VELOCITIES.index((s, t, 0))]]):
                    brim_send[slot_of(s), slot_of(t), n : n + 1, :] = value[y : y + 1]

    copies = []

    def plan(src, dst, offset):
        n = len(copies)
        copy = pltpu.make_async_remote_copy(
            src_ref=src, dst_ref=dst, send_sem=send_sem.at[n], recv_sem=recv_sem.at[n],
            device_id=device(offset), device_id_type=MESH,
        )
        copies.append(copy)
        return copy

    def send(src, dst, offset):
        plan(src, dst, offset).start()

    planned = [
        [plan(src.at[slot_of(s)], dst.at[slot_of(s)], (s, 0, 0)) for s in SIGNS]
        for src, dst in ((brim_send, brim_recv), (halo_send, halo_recv))
    ]

    def send_ends(pair, later):
        for n, s in enumerate(SIGNS):
            other = number(device((s, 0, 0)))
            mine = number((gx, gy, gz))

            @pl.when(other > mine if later else other < mine)
            def _():
                pair[n].start()

    for pair in planned:
        send_ends(pair, later=False)

    with jax.named_scope("p_middle"):
        for load in loads[7:]:
            load.wait()
        pl.loop(1, hx - 1)(prepare)

    def send_group(g):
        pl.semaphore_wait(ready_sem.at[g], jnp.minimum(per, (g + 1) * per - 1 - me))
        loop(jnp.maximum(me + 1, g * per), (g + 1) * per, send_beads)

    with jax.named_scope("p_barrier2"):
        @pl.when(me == 0)
        def _():
            pl.semaphore_wait(barrier, owners - 1 + lower)
            loop(0, owners - 1, lambda n: send_beads(owners - 1 - n))
            reply_cross()

        @pl.when(me > 0)
        def _():
            loop(lax.div(me + 1, per), tiles, send_group)

        send_ends(planned[0], later=True)

        @pl.when(lower < len(cross))
        def _():
            pl.semaphore_wait(cross_sem, len(cross) - lower)

    with jax.named_scope("p_csend"):
        pack_x(cstream, cxs, ces)
        for s in SIGNS:
            send(cxs.at[slot_of(s)], cxr.at[slot_of(s)], (s, 0, 0))
        pack_yz(cstream, cys, czs, ces)
        for s in SIGNS:
            send(cys.at[slot_of(s)], cyr.at[slot_of(s)], (0, s, 0))
            send(czs.at[slot_of(s)], czr.at[slot_of(s)], (0, 0, s))
        for n, i in enumerate(EDGES):
            send(ces.at[n], cer.at[n], VELOCITIES[i])
        for n in range(2):
            fzs[n] = jnp.zeros((ny, LANES), f32)
        send_ends(planned[1], later=True)
        force[...] = jnp.zeros_like(force)
        halo_force[...] = jnp.zeros_like(halo_force)

    bins_y, bins_z = ny // 2, nz // BIN_Z
    bins_xy = (nx // 2) * bins_y
    near = jnp.where(sub < per, 0, 1)

    def gathered(t, side_of, mine):
        source = [
            [
                jnp.broadcast_to(bead_recv[t * per + j, side_of, pl.ds(n, 1), :], (FIELDS, LANES))
                for n in range(FIELDS // per)
            ]
            for j in range(per)
        ]
        both = []
        for rows in source:
            value = rows[0]
            for n in range(1, FIELDS // per):
                value = jnp.where(sub >= n * per, rows[n], value)
            both.append(value)
        where = (diagonal + (per - mine)) & (per - 1)
        tile = None
        for m in range(per):
            mixed = both[m % per]
            for f in range(1, per):
                mixed = jnp.where(turn == f, both[(f + m) % per], mixed)
            if m:
                mixed = pltpu.roll(mixed, slots * m, 1)
            tile = mixed if tile is None else jnp.where(where == m, mixed, tile)
        return tile

    row_i = lax.div(sub, 2).astype(f32)
    row_j = (sub & 1).astype(f32)
    depth = lax.broadcasted_iota(jnp.int32, (BIN_Z, LANES), 0).astype(f32)
    own_rows = lax.broadcasted_iota(jnp.int32, (bins_xy, LANES), 0).astype(f32)
    side_rows = lax.broadcasted_iota(jnp.int32, (bins_y, LANES), 0).astype(f32)
    bf16 = jnp.bfloat16

    def product(t, side_of, first, spots, offset, count):
        mine = lax.rem(lax.rem(gx + (side_of + (ngx - 1)), ngx) * ngy + gy, per)
        tile = gathered(t, side_of, mine)
        number = tile[6:7]
        column = jnp.floor((number + 0.5) * (1.0 / bins_z))
        layer = number - column * bins_z
        dx, dy = first - tile[0:1], row_j - tile[1:2]
        weight = jnp.exp(-0.5 * (dx * dx + dy * dy))
        mask = spots + offset == column
        highs, lows = [], []
        for d in range(3):
            pushed = weight * tile[3 + d : 4 + d]
            high = pushed.astype(bf16).astype(f32)
            low = pushed - high
            for n in range(count):
                highs.append(jnp.where(mask, high[n : n + 1], 0.0))
                lows.append(jnp.where(mask, low[n : n + 1], 0.0))
        lh = jnp.concatenate(highs, axis=0).astype(bf16)
        ll = jnp.concatenate(lows, axis=0).astype(bf16)
        dz = depth - tile[2:3]
        fall = jnp.exp(-0.5 * (dz * dz))
        fh = fall.astype(bf16).astype(f32)
        fl = fall - fh
        rh = jnp.concatenate([jnp.where(layer == n, fh, 0.0) for n in range(bins_z)], axis=0)
        rl = jnp.concatenate([jnp.where(layer == n, fl, 0.0) for n in range(bins_z)], axis=0)
        rh, rl = rh.astype(bf16), rl.astype(bf16)
        return lax.dot_general(
            jnp.concatenate([lh, lh, ll], axis=1),
            jnp.concatenate([rh, rl, rh], axis=1),
            (((1,), (1,)), ((), ())),
            preferred_element_type=f32,
        )

    far = lax.div(2 * gx, ngx)

    with jax.named_scope("p_force"):
        @pl.loop(0, tiles)
        def _(n):
            near = lax.rem(n + jnp.minimum(me, 1), tiles)
            t = near + far * (tiles - 1 - n - near)
            arrived = bead_recv.at[pl.ds(t * per, per)]
            pltpu.make_async_copy(arrived, arrived, tile_sem.at[t]).wait()

            value = product(t, 1, row_i, own_rows, 0.0, 4)
            for d in range(3):
                for i in range(2):
                    for j in range(2):
                        for b in range(nx // 2):
                            start = ((d * 2 + i) * 2 + j) * bins_xy + b * bins_y
                            at = pl.ds((2 * b + i) * ny + j, bins_y, stride=2)
                            force[d, at, :] += value[start : start + bins_y]

            for h in range(2):
                first = float(1 - h)
                value = product(t, 2 * h, first, side_rows, first * (bins_xy - bins_y), 2)
                for d in range(3):
                    for j in range(2):
                        start = (d * 2 + j) * bins_y
                        at = pl.ds(j, bins_y, stride=2)
                        halo_force[h, d, at, :] += value[start : start + bins_y]

    wide_lane = lax.broadcasted_iota(jnp.int32, (ny, LANES), 1)

    def collided(p, rho, m, f):
        inv = 1.0 / rho
        u = [(v + 0.5 * w) * inv for v, w in zip(m, f)]
        return relax(
            p, rho, u, 1.0 - 1.0 / TAU_FINE, 1.0 / TAU_FINE, f, 1.0 - 0.5 / TAU_FINE
        )

    with jax.named_scope("p_hwait"):
        for copy in copies[:2]:
            copy.wait_recv()

    def made_of(rho, m, f):
        inv = 1.0 / rho
        u = [(v + 0.5 * w) * inv for v, w in zip(m, f)]
        return setup(rho, u, 1.0 / TAU_FINE, f, 1.0 - 0.5 / TAU_FINE)

    keep = 1.0 - 1.0 / TAU_FINE
    row_x = lax.broadcasted_iota(jnp.int32, (nx, nz), 0)

    def rows(n):
        sign = (1 - 2 * n).astype(f32)
        y = (ny - 1) * (1 - n)
        p = [pops[i, rows_at(y), :] for i in range(19)]
        made = made_of(*moments(p), [force[d, rows_at(y), :] for d in range(3)])
        ends = []
        for h in range(2):
            ends.append(
                made_of(
                    brim_recv[h, n, 0:1, :],
                    [brim_recv[h, n, 1 + d : 2 + d, :] for d in range(3)],
                    [halo_force[h, d, pl.ds(y, 1), :] for d in range(3)],
                )
            )
        for j, i in enumerate(FACE[1, 1]):
            c = VELOCITIES[i]
            other = FACE[1, -1][j]
            even, odd = halves(i, made)
            block = keep * jnp.where(n == 0, p[i], p[other]) + (even + sign * odd)
            if c[2]:
                block = pltpu.roll(block, (1 if c[2] > 0 else nz - 1) + n * (c[2] * (nz - 2)), 1)
            if c[0]:
                block = pltpu.roll(block, (1 if c[0] > 0 else nx - 1) + n * (c[0] * (nx - 2)), 0)
                for h in range(2):
                    even, odd = halves(i, ends[h])
                    end = keep * brim_recv[h, n, 4:5, :] + (even + sign * odd)
                    row = (nx - 1) * h
                    enters = n == (h if c[0] > 0 else 1 - h)
                    block = jnp.where((row_x == row) & enters, end, block)
            fys[n, j] = block

    with jax.named_scope("p_rows"):
        pl.loop(0, 2)(rows)
        for s in SIGNS:
            send(fys.at[slot_of(s)], fyr.at[slot_of(s)], (0, s, 0))
        for n, i in enumerate(EDGES_YZ):
            s = VELOCITIES[i][1]
            send(fys.at[slot_of(s), FACE[1, s].index(i)], fer.at[n], VELOCITIES[i])

    def collide(p, rho, m, f, x):
        post = collided(p, rho, m, f)
        columns = [fzs[n] for n in range(2)]
        for i in range(19):
            c = VELOCITIES[i]
            if post[i] is None:
                continue
            at = x + c[0] if isinstance(x, int) else lax.rem(x + (c[0] + nx), nx)
            plane = moved(post[i], (0, c[1], 0))
            stream[i, plane_at(at)] = moved(plane, (0, 0, c[2]))
            if c[2]:
                n = slot_of(c[2])
                k = FACE[2, c[2]].index(i) * nx + at
                turned = pltpu.roll(plane, lax.rem(k + (1 - n), LANES), 1)
                columns[n] = jnp.where(wide_lane == k, turned, columns[n])
        for n in range(2):
            fzs[n] = columns[n]

    def collide_own(x):
        p = [pops[i, plane_at(x)] for i in range(19)]
        rho, m = moments(p)
        collide(p, rho, m, [force[d, plane_at(x)] for d in range(3)], x)

    with jax.named_scope("p_collide"):
        pl.loop(0, nx)(collide_own)

    with jax.named_scope("p_hwait2"):
        for copy in copies[2:4]:
            copy.wait_recv()

    with jax.named_scope("p_hcollide"):
        for s in SIGNS:
            n = slot_of(s)
            p = [None] * 19
            for j, i in enumerate(FACE[0, s]):
                p[i] = halo_recv[n, 4 + j]
            collide(
                p, halo_recv[n, 0], [halo_recv[n, 1 + d] for d in range(3)],
                [halo_force[n, d] for d in range(3)], -1 if s > 0 else nx,
            )

    with jax.named_scope("p_sendz"):
        for s in SIGNS:
            send(fzs.at[slot_of(s)], fzr.at[slot_of(s)], (0, 0, s))

    with jax.named_scope("p_coarse"):
        for copy in copies[4:22]:
            copy.wait()
        fill_coarse(cstream, cxr, cyr, czr, cer)

    with jax.named_scope("p_ywait"):
        for copy in copies[22:28]:
            copy.wait()

    with jax.named_scope("p_yfill"):
        corner = lax.broadcasted_iota(jnp.int32, (nx, nz), 1)
        for s in SIGNS:
            for j, i in enumerate(FACE[1, s]):
                c = VELOCITIES[i]
                block = fyr[slot_of(s), j]
                if c[2]:
                    block = jnp.where(corner == side(c[2], nz), fer[EDGES_YZ.index(i)], block)
                stream[i, rows_at(side(s, ny)), :] = block

    with jax.named_scope("p_zwait"):
        for copy in copies[28:30]:
            copy.wait()

    with jax.named_scope("p_final"):
        sent = bead_recv.at[pl.ds(0, owners - 1)]
        pltpu.make_async_copy(sent, sent, bead_sem).wait()
        for copy in copies[:4]:
            copy.wait_send()


def local(populations, coarse_pops, fine_mask, coarse_mask, bead_data, bead_bins):
    _, nx, ny, nz = populations.shape
    _, hx, hy, hz = coarse_pops.shape
    sizes = tuple(lax.axis_size(axis) for axis in ("gx", "gy", "gz"))
    owners = sizes[0] * sizes[1]
    total = bead_data.shape[4]
    chunks = total // LANES
    slots = total // owners
    per = LANES // slots
    rows = FIELDS // per
    beads = bead_data.reshape(6 * chunks, LANES)
    bins = bead_bins.reshape(chunks, LANES)
    f32, i32 = jnp.float32, jnp.int32
    any_spec = pl.BlockSpec(memory_space=pl.ANY)
    hbm_spec = pl.BlockSpec(memory_space=pltpu.HBM)
    vmem_spec = pl.BlockSpec(memory_space=pltpu.VMEM)
    dma = pltpu.SemaphoreType.DMA

    fine_rim = [(2, 5, nx, nz), (2, ny, LANES), (len(EDGES_YZ), nx, nz)]
    coarse_rim = [(2, 5, hy, hz), (2, 5 * hx, 1, hz), (2, hy, LANES), (12, 1, LANES)]
    shapes = [(19, nx * ny, nz), (2, ny, LANES), coarse_pops.shape]
    vmem = [
        (3, nx * ny, nz), (2, 3, ny, nz),
        (2, 9, ny, nz), (2, 9, ny, nz), (2, 2, 8, nz), (2, 2, 8, nz),
        (FIELDS, LANES), (sizes[1], sizes[0] + 2, rows, LANES), (owners, 3, rows, LANES),
        *fine_rim[:2], *coarse_rim, fine_rim[0], fine_rim[2], *coarse_rim,
    ]
    operands = (
        populations.reshape(19, nx * ny, nz), coarse_pops, fine_mask, coarse_mask, beads, bins
    )
    fine, columns, coarse = pl.pallas_call(
        functools.partial(kernel, sizes, slots),
        out_shape=[jax.ShapeDtypeStruct(shape, f32) for shape in shapes],
        in_specs=[hbm_spec] * 6,
        out_specs=[vmem_spec, any_spec, vmem_spec],
        scratch_shapes=[
            pltpu.VMEM((19, nx * ny, nz), f32),
            pltpu.VMEM((19, hx, hy, hz), f32),
            pltpu.VMEM((nx, ny, nz), i32),
            pltpu.VMEM((hx, hy, hz), i32),
            pltpu.VMEM((6 * chunks, LANES), f32),
            pltpu.VMEM((chunks, LANES), i32),
            pltpu.VMEM((19, ny, nz), f32),
            *[pltpu.VMEM(shape, f32) for shape in vmem],
            dma((8,)),
            dma,
            dma((owners // per,)),
            pltpu.SemaphoreType.REGULAR((owners // per,)),
            pltpu.SemaphoreType.REGULAR,
            dma((30,)),
            dma((30,)),
        ],
        compiler_params=pltpu.CompilerParams(
            collective_id=0, has_side_effects=True, vmem_limit_bytes=LIMIT
        ),
    )(*[pltpu.with_memory_space_constraint(v, pltpu.HBM) for v in operands])
    fine, coarse = pl.pallas_call(
        functools.partial(finish, nx),
        out_shape=[jax.ShapeDtypeStruct(shape, f32) for shape in (shapes[0], shapes[2])],
        in_specs=[vmem_spec] * 3,
        out_specs=[any_spec] * 2,
        scratch_shapes=[pltpu.VMEM((10, nx * ny, nz), f32), dma((20,))],
        compiler_params=pltpu.CompilerParams(vmem_limit_bytes=LIMIT),
    )(fine, columns, coarse)
    return fine.reshape(populations.shape), coarse


def solution(mesh):
    in_specs = (
        P(None, "gx", "gy", "gz"),
        P(None, "gx", "gy", "gz"),
        P("gx", "gy", "gz"),
        P("gx", "gy", "gz"),
        P("gx", "gy", "gz", None, None),
        P("gx", "gy", "gz", None, None),
    )
    out_specs = (P(None, "gx", "gy", "gz"), P(None, "gx", "gy", "gz"))
    return jax.shard_map(local, mesh=mesh, in_specs=in_specs, out_specs=out_specs, check_vma=False)
```

time: 18.7 us -> 17 us (0.909)
  the two profiles are of different devices: /device:TPU:0 before, /device:TPU:29 now
where the time goes in v2:
time: 17 us; the launch traced here: 16.8 us
  Pallas kernels  16.1 us (95%)
  between operations  0.64 us (4%)
    pallas_call x1, Pallas kernels, local(): pl.pallas_call(functools.partial(kernel, sizes, slots), out_shape=[jax.Sh...  14.9 us
    pallas_call x1, Pallas kernels, local(): pl.pallas_call(functools.partial(finish, nx), out_shape=[jax.ShapeDtypeSt...  1.29 us

profile of v2, /device:TPU:29, one launch (start us, length us, event | category | flops | bytes accessed | tf_op | source)
XLA Modules:
  0.0 16.8 jit_solution(10258622371627151213)
XLA Ops:
  0.6 14.9 %shard_map.77 = (f32[19,128,128]{2,1,0:T(8,128)S(1)}, f32[2,16,128]{2,1,0:T(8,128)S(1)}, f32[19,4,8,64]{3,2,1,0:T(8,128)S(1)}) custom-call(f32[19,128,128]{2,1,0:T(8,128)} %bitcast.4, f32[19,4,8,64]{3,2,1,0:T(8,128)} %cpop_in.1, s32[8,16,128]{2,1,0:T(8,128)} %fmask_in.1, s32[4,8,64]{2,1,0:T(8,128)} %cmask_in.1, f32[24,128]{1,0:T(8,128)} %bitcast.5, ...), custom_call_target="tpu_custom_call" | custom-call | tf_op jit(solution)/shard_map/pallas_call | solution.py:796
  15.5 1.3 %shard_map.78 = (f32[19,128,128]{2,1,0:T(8,128)}, f32[19,4,8,64]{3,2,1,0:T(8,128)}) custom-call(f32[19,128,128]{2,1,0:T(8,128)S(1)} %get-tuple-element.7.fine, f32[2,16,128]{2,1,0:T(8,128)S(1)} %get-tuple-element.8.columns, f32[19,4,8,64]{3,2,1,0:T(8,128)S(1)} %get-tuple-element.9.coarse), custom_call_target="tpu_custom_call" | custom-call | tf_op jit(solution)/shard_map/pallas_call | solution.py:822

commit v3 on v2

--- a/solution.py
+++ b/solution.py
@@ -197,13 +197,12 @@
 def finish(nx, fine, columns, coarse, fine_out, coarse_out, target, store_sem):
     _, height, nz = fine.shape
     ny = height // nx
-    order = [i for i in range(19) if not VELOCITIES[i][2]]
-    turned = [i for i in range(19) if VELOCITIES[i][2]]
-    stores = [pltpu.make_async_copy(coarse, coarse_out, store_sem.at[19])]
-    for i in order + turned:
-        source = target.at[turned.index(i)] if i in turned else fine.at[i]
-        stores.append(pltpu.make_async_copy(source, fine_out.at[i], store_sem.at[i]))
-    for store in stores[: 1 + len(order)]:
+    turned = [5, 6, *range(11, 19)]
+    parts = [(coarse, coarse_out), (fine.at[0:5], fine_out.at[0:5]), (fine.at[7:11], fine_out.at[7:11])]
+    for n in range(0, 10, 2):
+        parts.append((target.at[n : n + 2], fine_out.at[turned[n] : turned[n] + 2]))
+    stores = [pltpu.make_async_copy(src, dst, store_sem.at[n]) for n, (src, dst) in enumerate(parts)]
+    for store in stores[:3]:
         store.start()
     last = lax.broadcasted_iota(jnp.int32, (ny, nz), 1)
     row = lax.broadcasted_iota(jnp.int32, (ny, nz), 0)
@@ -218,7 +217,8 @@
             target[n, x * ny : (x + 1) * ny, :] = jnp.where(
                 spot, column[:, k : k + 1], fine[i, x * ny : (x + 1) * ny, :]
             )
-        stores[1 + len(order) + n].start()
+        if n % 2:
+            stores[3 + n // 2].start()
     for store in stores:
         store.wait()
 
@@ -236,7 +236,7 @@
     stream, fzr, cstream,
     pops, cpops, fmask, cmask, bead_ref, bins_ref, tall,
     force, halo_force, halo_send, halo_recv, brim_send, brim_recv,
-    bead_rows, bead_send, bead_recv, fys, fzs, cxs, cys, czs, ces,
+    bead_rows, bead_send, bead_recv, fys, fzs, fxs, fxr, cxs, cys, czs, ces,
     fyr, fer, cxr, cyr, czr, cer,
     in_sem, bead_sem, tile_sem, ready_sem, cross_sem, send_sem, recv_sem,
 ):
@@ -251,15 +251,23 @@
     tiles = owners // per
     f32 = jnp.float32
 
-    ends = [(0, 2), (nx - 2, 2)]
-    middle = [(2, nx - 4)]
+    barrier = pltpu.get_barrier_semaphore()
+    half = tiles // 2
+    late = me >= half * per
+
+    @pl.when(late & (me > 0))
+    def _():
+        pl.semaphore_signal(barrier, inc=1, device_id=(0, 0, gz), device_id_type=MESH)
+
+    def part(x, w):
+        return pop_in.at[:, pl.ds(x * ny, w * ny)], pops.at[:, pl.ds(x * ny, w * ny)]
+
     loads = [
         pltpu.make_async_copy(src, dst, in_sem.at[n])
-        for n, (src, dst) in enumerate(
-            [(bead_in, bead_ref), (bins_in, bins_ref)]
-            + [(pop_in.at[:, pl.ds(x * ny, w * ny)], pops.at[:, pl.ds(x * ny, w * ny)]) for x, w in ends]
-            + [(cmask_in, cmask), (fmask_in, fmask), (cpop_in, cpops)]
-            + [(pop_in.at[:, pl.ds(x * ny, w * ny)], pops.at[:, pl.ds(x * ny, w * ny)]) for x, w in middle]
+        for n, src, dst in (
+            (0, bead_in, bead_ref), (1, bins_in, bins_ref), (2, *part(0, 2)), (2, *part(nx - 2, 2)),
+            (3, cmask_in, cmask), (4, fmask_in, fmask), (5, cpop_in, cpops),
+            (6, *part(2, nx - 4)),
         )
     ]
     for load in loads:
@@ -297,7 +305,6 @@
     def loop(start, stop, act):
         lax.fori_loop(start, stop, lambda n, carry: (act(n), carry)[1], 0)
 
-    barrier = pltpu.get_barrier_semaphore()
     cross = [(0, 0, 1), (0, 0, -1)] + [VELOCITIES[i] for i in EDGES if VELOCITIES[i][2]]
     lower = jnp.int32(0)
     for offset in cross:
@@ -310,11 +317,6 @@
                 barrier, inc=1, device_id=place(owners - 1 - n), device_id_type=MESH
             ),
         )
-
-        @pl.when(me > 0)
-        def _():
-            pl.semaphore_signal(barrier, inc=1, device_id=place(0), device_id_type=MESH)
-
         cross_peers(
             lambda where: pl.semaphore_signal(
                 barrier, inc=1, device_id=where, device_id_type=MESH
@@ -355,7 +357,7 @@
         def _():
             pl.semaphore_wait(barrier, me + lower)
             loop(
-                1, me,
+                late.astype(jnp.int32), me,
                 lambda o: pl.semaphore_signal(
                     ready_sem.at[me // per], inc=1, device_id=place(o), device_id_type=MESH
                 ),
@@ -444,7 +446,8 @@
                 pops[q, at] = jnp.where(kept, pops[q, at], tall[q])
 
     with jax.named_scope("p_ends"):
-        for load in loads[2:7]:
+        pltpu.make_async_copy(*part(0, 4), in_sem.at[2]).wait()
+        for load in loads[4:7]:
             load.wait()
         pl.loop(0, 2)(lambda n: prepare(n * (hx - 1)))
         for s in SIGNS:
@@ -458,36 +461,44 @@
                 for n, value in enumerate([rho, *m, p[VELOCITIES.index((s, t, 0))]]):
                     brim_send[slot_of(s), slot_of(t), n : n + 1, :] = value[y : y + 1]
 
-    copies = []
-
-    def plan(src, dst, offset):
-        n = len(copies)
-        copy = pltpu.make_async_remote_copy(
-            src_ref=src, dst_ref=dst, send_sem=send_sem.at[n], recv_sem=recv_sem.at[n],
+    BRIM, HALO, COARSE_X, COARSE_Y, COARSE_Z, COARSE_EDGE, ROWS, CORNERS, ENDS, COLUMNS = range(10)
+    buffers = [
+        (brim_send, brim_recv), (halo_send, halo_recv),
+        (cxs, cxr), (cys, cyr), (czs, czr), (ces, cer),
+        (fys, fyr), (fer, fer), (fxs, fxr), (fzs, fzr),
+    ]
+
+    def plan(kind, src, dst, offset):
+        return pltpu.make_async_remote_copy(
+            src_ref=src, dst_ref=dst, send_sem=send_sem.at[kind], recv_sem=recv_sem.at[kind],
             device_id=device(offset), device_id_type=MESH,
         )
-        copies.append(copy)
-        return copy
-
-    def send(src, dst, offset):
-        plan(src, dst, offset).start()
-
-    planned = [
-        [plan(src.at[slot_of(s)], dst.at[slot_of(s)], (s, 0, 0)) for s in SIGNS]
-        for src, dst in ((brim_send, brim_recv), (halo_send, halo_recv))
-    ]
-
-    def send_ends(pair, later):
-        for n, s in enumerate(SIGNS):
+
+    def send(kind, part, offset):
+        src, dst = buffers[kind]
+        plan(kind, src.at[part], dst.at[part], offset).start()
+
+    def arrive(*kinds):
+        for kind in kinds:
+            dst = buffers[kind][1]
+            pltpu.make_async_copy(dst, dst, recv_sem.at[kind]).wait()
+
+    def leave(*kinds):
+        for kind in kinds:
+            src = buffers[kind][0]
+            pltpu.make_async_copy(src, src, send_sem.at[kind]).wait()
+
+    def send_ends(kind, later):
+        for s in SIGNS:
             other = number(device((s, 0, 0)))
             mine = number((gx, gy, gz))
 
             @pl.when(other > mine if later else other < mine)
             def _():
-                pair[n].start()
-
-    for pair in planned:
-        send_ends(pair, later=False)
+                send(kind, slot_of(s), (s, 0, 0))
+
+    send_ends(BRIM, later=False)
+    send_ends(HALO, later=False)
 
     with jax.named_scope("p_middle"):
         for load in loads[7:]:
@@ -501,15 +512,17 @@
     with jax.named_scope("p_barrier2"):
         @pl.when(me == 0)
         def _():
-            pl.semaphore_wait(barrier, owners - 1 + lower)
-            loop(0, owners - 1, lambda n: send_beads(owners - 1 - n))
+            loop(0, half, send_group)
+            pl.semaphore_wait(barrier, owners - max(1, half * per) + lower)
+            first = max(1, half * per)
+            loop(0, owners - first, lambda n: send_beads(owners - 1 - n))
             reply_cross()
 
         @pl.when(me > 0)
         def _():
             loop(lax.div(me + 1, per), tiles, send_group)
 
-        send_ends(planned[0], later=True)
+        send_ends(BRIM, later=True)
 
         @pl.when(lower < len(cross))
         def _():
@@ -518,16 +531,16 @@
     with jax.named_scope("p_csend"):
         pack_x(cstream, cxs, ces)
         for s in SIGNS:
-            send(cxs.at[slot_of(s)], cxr.at[slot_of(s)], (s, 0, 0))
+            send(COARSE_X, slot_of(s), (s, 0, 0))
         pack_yz(cstream, cys, czs, ces)
         for s in SIGNS:
-            send(cys.at[slot_of(s)], cyr.at[slot_of(s)], (0, s, 0))
-            send(czs.at[slot_of(s)], czr.at[slot_of(s)], (0, 0, s))
+            send(COARSE_Y, slot_of(s), (0, s, 0))
+            send(COARSE_Z, slot_of(s), (0, 0, s))
         for n, i in enumerate(EDGES):
-            send(ces.at[n], cer.at[n], VELOCITIES[i])
+            send(COARSE_EDGE, n, VELOCITIES[i])
         for n in range(2):
             fzs[n] = jnp.zeros((ny, LANES), f32)
-        send_ends(planned[1], later=True)
+        send_ends(HALO, later=True)
         force[...] = jnp.zeros_like(force)
         halo_force[...] = jnp.zeros_like(halo_force)
 
@@ -637,32 +650,18 @@
             p, rho, u, 1.0 - 1.0 / TAU_FINE, 1.0 / TAU_FINE, f, 1.0 - 0.5 / TAU_FINE
         )
 
-    with jax.named_scope("p_hwait"):
-        for copy in copies[:2]:
-            copy.wait_recv()
-
     def made_of(rho, m, f):
         inv = 1.0 / rho
         u = [(v + 0.5 * w) * inv for v, w in zip(m, f)]
         return setup(rho, u, 1.0 / TAU_FINE, f, 1.0 - 0.5 / TAU_FINE)
 
     keep = 1.0 - 1.0 / TAU_FINE
-    row_x = lax.broadcasted_iota(jnp.int32, (nx, nz), 0)
 
     def rows(n):
         sign = (1 - 2 * n).astype(f32)
         y = (ny - 1) * (1 - n)
         p = [pops[i, rows_at(y), :] for i in range(19)]
         made = made_of(*moments(p), [force[d, rows_at(y), :] for d in range(3)])
-        ends = []
-        for h in range(2):
-            ends.append(
-                made_of(
-                    brim_recv[h, n, 0:1, :],
-                    [brim_recv[h, n, 1 + d : 2 + d, :] for d in range(3)],
-                    [halo_force[h, d, pl.ds(y, 1), :] for d in range(3)],
-                )
-            )
         for j, i in enumerate(FACE[1, 1]):
             c = VELOCITIES[i]
             other = FACE[1, -1][j]
@@ -672,21 +671,39 @@
                 block = pltpu.roll(block, (1 if c[2] > 0 else nz - 1) + n * (c[2] * (nz - 2)), 1)
             if c[0]:
                 block = pltpu.roll(block, (1 if c[0] > 0 else nx - 1) + n * (c[0] * (nx - 2)), 0)
-                for h in range(2):
-                    even, odd = halves(i, ends[h])
-                    end = keep * brim_recv[h, n, 4:5, :] + (even + sign * odd)
-                    row = (nx - 1) * h
-                    enters = n == (h if c[0] > 0 else 1 - h)
-                    block = jnp.where((row_x == row) & enters, end, block)
             fys[n, j] = block
 
     with jax.named_scope("p_rows"):
         pl.loop(0, 2)(rows)
         for s in SIGNS:
-            send(fys.at[slot_of(s)], fyr.at[slot_of(s)], (0, s, 0))
+            send(ROWS, slot_of(s), (0, s, 0))
         for n, i in enumerate(EDGES_YZ):
             s = VELOCITIES[i][1]
-            send(fys.at[slot_of(s), FACE[1, s].index(i)], fer.at[n], VELOCITIES[i])
+            block = fys.at[slot_of(s), FACE[1, s].index(i)]
+            plan(CORNERS, block, fer.at[n], VELOCITIES[i]).start()
+
+    def end_rows(n):
+        sign = (1 - 2 * n).astype(f32)
+        y = (ny - 1) * (1 - n)
+        for h in range(2):
+            made = made_of(
+                brim_recv[h, n, 0:1, :],
+                [brim_recv[h, n, 1 + d : 2 + d, :] for d in range(3)],
+                [halo_force[h, d, pl.ds(y, 1), :] for d in range(3)],
+            )
+            both = [halves(VELOCITIES.index((s, 1, 0)), made) for s in SIGNS]
+            straight = n == h
+            even = jnp.where(straight, both[0][0], both[1][0])
+            odd = jnp.where(straight, both[0][1], both[1][1])
+            fxs[n, h : h + 1, :] = keep * brim_recv[h, n, 4:5, :] + (even + sign * odd)
+
+    with jax.named_scope("p_hwait"):
+        arrive(BRIM)
+
+    with jax.named_scope("p_endrows"):
+        pl.loop(0, 2)(end_rows)
+        for s in SIGNS:
+            send(ENDS, slot_of(s), (0, s, 0))
 
     def collide(p, rho, m, f, x):
         post = collided(p, rho, m, f)
@@ -715,8 +732,7 @@
         pl.loop(0, nx)(collide_own)
 
     with jax.named_scope("p_hwait2"):
-        for copy in copies[2:4]:
-            copy.wait_recv()
+        arrive(HALO)
 
     with jax.named_scope("p_hcollide"):
         for s in SIGNS:
@@ -731,36 +747,37 @@
 
     with jax.named_scope("p_sendz"):
         for s in SIGNS:
-            send(fzs.at[slot_of(s)], fzr.at[slot_of(s)], (0, 0, s))
+            send(COLUMNS, slot_of(s), (0, 0, s))
 
     with jax.named_scope("p_coarse"):
-        for copy in copies[4:22]:
-            copy.wait()
+        arrive(COARSE_X, COARSE_Y, COARSE_Z, COARSE_EDGE)
         fill_coarse(cstream, cxr, cyr, czr, cer)
 
     with jax.named_scope("p_ywait"):
-        for copy in copies[22:28]:
-            copy.wait()
+        arrive(ROWS, CORNERS, ENDS)
 
     with jax.named_scope("p_yfill"):
         corner = lax.broadcasted_iota(jnp.int32, (nx, nz), 1)
+        row_x = lax.broadcasted_iota(jnp.int32, (nx, nz), 0)
         for s in SIGNS:
             for j, i in enumerate(FACE[1, s]):
                 c = VELOCITIES[i]
                 block = fyr[slot_of(s), j]
                 if c[2]:
                     block = jnp.where(corner == side(c[2], nz), fer[EDGES_YZ.index(i)], block)
+                if c[0]:
+                    h = slot_of(c[0])
+                    end = fxr[slot_of(s), h : h + 1, :]
+                    block = jnp.where(row_x == side(c[0], nx), end, block)
                 stream[i, rows_at(side(s, ny)), :] = block
 
     with jax.named_scope("p_zwait"):
-        for copy in copies[28:30]:
-            copy.wait()
+        arrive(COLUMNS)
 
     with jax.named_scope("p_final"):
         sent = bead_recv.at[pl.ds(0, owners - 1)]
         pltpu.make_async_copy(sent, sent, bead_sem).wait()
-        for copy in copies[:4]:
-            copy.wait_send()
+        leave(*range(10))
 
 
 def local(populations, coarse_pops, fine_mask, coarse_mask, bead_data, bead_bins):
@@ -788,7 +805,7 @@
         (3, nx * ny, nz), (2, 3, ny, nz),
         (2, 9, ny, nz), (2, 9, ny, nz), (2, 2, 8, nz), (2, 2, 8, nz),
         (FIELDS, LANES), (sizes[1], sizes[0] + 2, rows, LANES), (owners, 3, rows, LANES),
-        *fine_rim[:2], *coarse_rim, fine_rim[0], fine_rim[2], *coarse_rim,
+        *fine_rim[:2], (2, 2, nz), (2, 2, nz), *coarse_rim, fine_rim[0], fine_rim[2], *coarse_rim,
     ]
     operands = (
         populations.reshape(19, nx * ny, nz), coarse_pops, fine_mask, coarse_mask, beads, bins
@@ -807,13 +824,13 @@
             pltpu.VMEM((chunks, LANES), i32),
             pltpu.VMEM((19, ny, nz), f32),
             *[pltpu.VMEM(shape, f32) for shape in vmem],
-            dma((8,)),
+            dma((7,)),
             dma,
             dma((owners // per,)),
             pltpu.SemaphoreType.REGULAR((owners // per,)),
             pltpu.SemaphoreType.REGULAR,
-            dma((30,)),
-            dma((30,)),
+            dma((10,)),
+            dma((10,)),
         ],
         compiler_params=pltpu.CompilerParams(
             collective_id=0, has_side_effects=True, vmem_limit_bytes=LIMIT
@@ -824,7 +841,7 @@
         out_shape=[jax.ShapeDtypeStruct(shape, f32) for shape in (shapes[0], shapes[2])],
         in_specs=[vmem_spec] * 3,
         out_specs=[any_spec] * 2,
-        scratch_shapes=[pltpu.VMEM((10, nx * ny, nz), f32), dma((20,))],
+        scratch_shapes=[pltpu.VMEM((10, nx * ny, nz), f32), dma((8,))],
         compiler_params=pltpu.CompilerParams(vmem_limit_bytes=LIMIT),
     )(fine, columns, coarse)
     return fine.reshape(populations.shape), coarse

time: 17 us -> 16.6 us (0.976)
  the two profiles are of different devices: /device:TPU:29 before, /device:TPU:0 now
where the time goes in v3:
time: 16.6 us; the launch traced here: 16.3 us
  Pallas kernels  15.6 us (94%)
  between operations  0.64 us (4%)
    pallas_call x1, Pallas kernels, local(): pl.pallas_call(functools.partial(kernel, sizes, slots), out_shape=[jax.Sh...  14.4 us
    pallas_call x1, Pallas kernels, local(): pl.pallas_call(functools.partial(finish, nx), out_shape=[jax.ShapeDtypeSt...  1.2 us

profile of v3, /device:TPU:0, one launch (start us, length us, event | category | flops | bytes accessed | tf_op | source)
XLA Modules:
  0.0 16.3 jit_solution(6826944797128340922)
XLA Ops:
  0.6 14.4 %shard_map.77 = (f32[19,128,128]{2,1,0:T(8,128)S(1)}, f32[2,16,128]{2,1,0:T(8,128)S(1)}, f32[19,4,8,64]{3,2,1,0:T(8,128)S(1)}) custom-call(f32[19,128,128]{2,1,0:T(8,128)} %bitcast.4, f32[19,4,8,64]{3,2,1,0:T(8,128)} %cpop_in.1, s32[8,16,128]{2,1,0:T(8,128)} %fmask_in.1, s32[4,8,64]{2,1,0:T(8,128)} %cmask_in.1, f32[24,128]{1,0:T(8,128)} %bitcast.5, ...), custom_call_target="tpu_custom_call" | custom-call | tf_op jit(solution)/shard_map/pallas_call | solution.py:813
  15.1 1.2 %shard_map.78 = (f32[19,128,128]{2,1,0:T(8,128)}, f32[19,4,8,64]{3,2,1,0:T(8,128)}) custom-call(f32[19,128,128]{2,1,0:T(8,128)S(1)} %get-tuple-element.7.fine, f32[2,16,128]{2,1,0:T(8,128)S(1)} %get-tuple-element.8.columns, f32[19,4,8,64]{3,2,1,0:T(8,128)S(1)} %get-tuple-element.9.coarse), custom_call_target="tpu_custom_call" | custom-call | tf_op jit(solution)/shard_map/pallas_call | solution.py:839

commit v4 on v3

--- a/solution.py
+++ b/solution.py
@@ -252,12 +252,18 @@
     f32 = jnp.float32
 
     barrier = pltpu.get_barrier_semaphore()
-    half = tiles // 2
-    late = me >= half * per
-
-    @pl.when(late & (me > 0))
-    def _():
-        pl.semaphore_signal(barrier, inc=1, device_id=(0, 0, gz), device_id_type=MESH)
+    first = me < per
+
+    def loop(start, stop, act):
+        lax.fori_loop(start, stop, lambda n, carry: (act(n), carry)[1], 0)
+
+    def place(o):
+        return lax.div(o, ngy), lax.rem(o, ngy), gz
+
+    def greet(o):
+        pl.semaphore_signal(barrier, inc=1, device_id=place(o), device_id_type=MESH)
+
+    loop(0, jnp.minimum(me, per), greet)
 
     def part(x, w):
         return pop_in.at[:, pl.ds(x * ny, w * ny)], pops.at[:, pl.ds(x * ny, w * ny)]
@@ -286,9 +292,6 @@
             lax.rem(gz + (offset[2] + ngz), ngz),
         )
 
-    def place(o):
-        return lax.div(o, ngy), lax.rem(o, ngy), gz
-
     def number(where):
         return (where[0] * ngy + where[1]) * ngz + where[2]
 
@@ -302,21 +305,18 @@
             def _():
                 act(where)
 
-    def loop(start, stop, act):
-        lax.fori_loop(start, stop, lambda n, carry: (act(n), carry)[1], 0)
-
     cross = [(0, 0, 1), (0, 0, -1)] + [VELOCITIES[i] for i in EDGES if VELOCITIES[i][2]]
     lower = jnp.int32(0)
     for offset in cross:
         lower = lower + (number(device(offset)) < number((gx, gy, gz))).astype(jnp.int32)
 
     with jax.named_scope("p_signals"):
-        loop(
-            0, owners - 1 - me,
-            lambda n: pl.semaphore_signal(
-                barrier, inc=1, device_id=place(owners - 1 - n), device_id_type=MESH
-            ),
-        )
+        loop(0, owners - jnp.maximum(per, me + 1), lambda n: greet(owners - 1 - n))
+
+        @pl.when(first)
+        def _():
+            loop(me + 1, per, greet)
+
         cross_peers(
             lambda where: pl.semaphore_signal(
                 barrier, inc=1, device_id=where, device_id_type=MESH
@@ -352,17 +352,6 @@
             for n, part in enumerate(block):
                 bead_send[b, a + 1, pl.ds(n, 1), :] = part
 
-    with jax.named_scope("p_barrier"):
-        @pl.when(me > 0)
-        def _():
-            pl.semaphore_wait(barrier, me + lower)
-            loop(
-                late.astype(jnp.int32), me,
-                lambda o: pl.semaphore_signal(
-                    ready_sem.at[me // per], inc=1, device_id=place(o), device_id_type=MESH
-                ),
-            )
-
     with jax.named_scope("p_pack"):
         for load in loads[:2]:
             load.wait()
@@ -376,6 +365,17 @@
         )
         own_beads.start()
 
+    with jax.named_scope("p_barrier"):
+        @pl.when(jnp.logical_not(first))
+        def _():
+            pl.semaphore_wait(barrier, me + lower)
+            loop(
+                per, me,
+                lambda o: pl.semaphore_signal(
+                    ready_sem.at[me // per], inc=1, device_id=place(o), device_id_type=MESH
+                ),
+            )
+
     def send_beads(o):
         where = place(o)
         pltpu.make_async_remote_copy(
@@ -396,7 +396,7 @@
         )
 
     with jax.named_scope("p_answer"):
-        @pl.when(me > 0)
+        @pl.when(jnp.logical_not(first))
         def _():
             loop(0, me, send_beads)
             reply_cross()
@@ -468,11 +468,14 @@
         (fys, fyr), (fer, fer), (fxs, fxr), (fzs, fzr),
     ]
 
-    def plan(kind, src, dst, offset):
+    def move(kind, src, dst, where):
         return pltpu.make_async_remote_copy(
             src_ref=src, dst_ref=dst, send_sem=send_sem.at[kind], recv_sem=recv_sem.at[kind],
-            device_id=device(offset), device_id_type=MESH,
+            device_id=where, device_id_type=MESH,
         )
+
+    def plan(kind, src, dst, offset):
+        return move(kind, src, dst, device(offset))
 
     def send(kind, part, offset):
         src, dst = buffers[kind]
@@ -488,8 +491,8 @@
             src = buffers[kind][0]
             pltpu.make_async_copy(src, src, send_sem.at[kind]).wait()
 
-    def send_ends(kind, later):
-        for s in SIGNS:
+    def send_ends(kind, later, signs=SIGNS):
+        for s in signs:
             other = number(device((s, 0, 0)))
             mine = number((gx, gy, gz))
 
@@ -497,8 +500,10 @@
             def _():
                 send(kind, slot_of(s), (s, 0, 0))
 
-    send_ends(BRIM, later=False)
-    send_ends(HALO, later=False)
+    @pl.when(jnp.logical_not(first))
+    def _():
+        send_ends(BRIM, later=False)
+        send_ends(HALO, later=False)
 
     with jax.named_scope("p_middle"):
         for load in loads[7:]:
@@ -510,15 +515,16 @@
         loop(jnp.maximum(me + 1, g * per), (g + 1) * per, send_beads)
 
     with jax.named_scope("p_barrier2"):
-        @pl.when(me == 0)
+        @pl.when(first)
         def _():
-            loop(0, half, send_group)
-            pl.semaphore_wait(barrier, owners - max(1, half * per) + lower)
-            first = max(1, half * per)
-            loop(0, owners - first, lambda n: send_beads(owners - 1 - n))
+            pl.semaphore_wait(barrier, owners - 1 + lower)
+            loop(0, me, send_beads)
+            loop(me + 1, owners, send_beads)
             reply_cross()
-
-        @pl.when(me > 0)
+            send_ends(BRIM, later=False)
+            send_ends(HALO, later=False)
+
+        @pl.when(jnp.logical_not(first))
         def _():
             loop(lax.div(me + 1, per), tiles, send_group)
 
@@ -540,7 +546,7 @@
             send(COARSE_EDGE, n, VELOCITIES[i])
         for n in range(2):
             fzs[n] = jnp.zeros((ny, LANES), f32)
-        send_ends(HALO, later=True)
+        send_ends(HALO, later=True, signs=(1,))
         force[...] = jnp.zeros_like(force)
         halo_force[...] = jnp.zeros_like(halo_force)
 
@@ -618,7 +624,7 @@
     with jax.named_scope("p_force"):
         @pl.loop(0, tiles)
         def _(n):
-            near = lax.rem(n + jnp.minimum(me, 1), tiles)
+            near = (1 - lax.div(n + 2, tiles)) * (n + 1) + lax.div(n + 1, tiles) * (tiles - 1)
             t = near + far * (tiles - 1 - n - near)
             arrived = bead_recv.at[pl.ds(t * per, per)]
             pltpu.make_async_copy(arrived, arrived, tile_sem.at[t]).wait()
@@ -640,6 +646,8 @@
                         start = (d * 2 + j) * bins_y
                         at = pl.ds(j, bins_y, stride=2)
                         halo_force[h, d, at, :] += value[start : start + bins_y]
+
+    send_ends(HALO, later=True, signs=(-1,))
 
     wide_lane = lax.broadcasted_iota(jnp.int32, (ny, LANES), 1)
 
@@ -672,11 +680,11 @@
             if c[0]:
                 block = pltpu.roll(block, (1 if c[0] > 0 else nx - 1) + n * (c[0] * (nx - 2)), 0)
             fys[n, j] = block
+        where = (gx, lax.rem(gy + (1 - 2 * n) + ngy, ngy), gz)
+        move(ROWS, fys.at[n], fyr.at[n], where).start()
 
     with jax.named_scope("p_rows"):
         pl.loop(0, 2)(rows)
-        for s in SIGNS:
-            send(ROWS, slot_of(s), (0, s, 0))
         for n, i in enumerate(EDGES_YZ):
             s = VELOCITIES[i][1]
             block = fys.at[slot_of(s), FACE[1, s].index(i)]

time: 16.6 us -> 16.2 us (0.976)
  Pallas kernels: 15.6 us -> 15.3 us
    pallas_call x1, Pallas kernels: 14.4 us -> 14.1 us  [local(): pl.pallas_call(functools.partial(kernel, sizes, slots), out_shape=[jax.Sh...]
where the time goes in v4:
time: 16.2 us; the launch traced here: 16 us
  Pallas kernels  15.3 us (94%)
  between operations  0.64 us (4%)
    pallas_call x1, Pallas kernels, local(): pl.pallas_call(functools.partial(kernel, sizes, slots), out_shape=[jax.Sh...  14.1 us
    pallas_call x1, Pallas kernels, local(): pl.pallas_call(functools.partial(finish, nx), out_shape=[jax.ShapeDtypeSt...  1.2 us

profile of v4, /device:TPU:0, one launch (start us, length us, event | category | flops | bytes accessed | tf_op | source)
XLA Modules:
  0.0 16.0 jit_solution(6665072104540723244)
XLA Ops:
  0.6 14.1 %shard_map.77 = (f32[19,128,128]{2,1,0:T(8,128)S(1)}, f32[2,16,128]{2,1,0:T(8,128)S(1)}, f32[19,4,8,64]{3,2,1,0:T(8,128)S(1)}) custom-call(f32[19,128,128]{2,1,0:T(8,128)} %bitcast.4, f32[19,4,8,64]{3,2,1,0:T(8,128)} %cpop_in.1, s32[8,16,128]{2,1,0:T(8,128)} %fmask_in.1, s32[4,8,64]{2,1,0:T(8,128)} %cmask_in.1, f32[24,128]{1,0:T(8,128)} %bitcast.5, ...), custom_call_target="tpu_custom_call" | custom-call | tf_op jit(solution)/shard_map/pallas_call | solution.py:821
  14.8 1.2 %shard_map.78 = (f32[19,128,128]{2,1,0:T(8,128)}, f32[19,4,8,64]{3,2,1,0:T(8,128)}) custom-call(f32[19,128,128]{2,1,0:T(8,128)S(1)} %get-tuple-element.7.fine, f32[2,16,128]{2,1,0:T(8,128)S(1)} %get-tuple-element.8.columns, f32[19,4,8,64]{3,2,1,0:T(8,128)S(1)} %get-tuple-element.9.coarse), custom_call_target="tpu_custom_call" | custom-call | tf_op jit(solution)/shard_map/pallas_call | solution.py:847

commit v5 on v4

--- a/solution.py
+++ b/solution.py
@@ -252,7 +252,8 @@
     f32 = jnp.float32
 
     barrier = pltpu.get_barrier_semaphore()
-    first = me < per
+    heads = ngy
+    first = me < heads
 
     def loop(start, stop, act):
         lax.fori_loop(start, stop, lambda n, carry: (act(n), carry)[1], 0)
@@ -263,7 +264,7 @@
     def greet(o):
         pl.semaphore_signal(barrier, inc=1, device_id=place(o), device_id_type=MESH)
 
-    loop(0, jnp.minimum(me, per), greet)
+    loop(0, jnp.minimum(me, heads), greet)
 
     def part(x, w):
         return pop_in.at[:, pl.ds(x * ny, w * ny)], pops.at[:, pl.ds(x * ny, w * ny)]
@@ -311,11 +312,11 @@
         lower = lower + (number(device(offset)) < number((gx, gy, gz))).astype(jnp.int32)
 
     with jax.named_scope("p_signals"):
-        loop(0, owners - jnp.maximum(per, me + 1), lambda n: greet(owners - 1 - n))
+        loop(0, owners - jnp.maximum(heads, me + 1), lambda n: greet(owners - 1 - n))
 
         @pl.when(first)
         def _():
-            loop(me + 1, per, greet)
+            loop(me + 1, heads, greet)
 
         cross_peers(
             lambda where: pl.semaphore_signal(
@@ -365,17 +366,6 @@
         )
         own_beads.start()
 
-    with jax.named_scope("p_barrier"):
-        @pl.when(jnp.logical_not(first))
-        def _():
-            pl.semaphore_wait(barrier, me + lower)
-            loop(
-                per, me,
-                lambda o: pl.semaphore_signal(
-                    ready_sem.at[me // per], inc=1, device_id=place(o), device_id_type=MESH
-                ),
-            )
-
     def send_beads(o):
         where = place(o)
         pltpu.make_async_remote_copy(
@@ -395,10 +385,18 @@
             later=False,
         )
 
-    with jax.named_scope("p_answer"):
+    with jax.named_scope("p_barrier"):
         @pl.when(jnp.logical_not(first))
         def _():
-            loop(0, me, send_beads)
+            pl.semaphore_wait(barrier, me + lower)
+            loop(0, heads, send_beads)
+            loop(
+                heads, me,
+                lambda o: pl.semaphore_signal(
+                    ready_sem.at[me // per], inc=1, device_id=place(o), device_id_type=MESH
+                ),
+            )
+            loop(heads, me, send_beads)
             reply_cross()
 
     fold = lax.broadcasted_iota(jnp.int32, (nz, hz), 0) - 2 * lax.broadcasted_iota(
@@ -586,7 +584,7 @@
     side_rows = lax.broadcasted_iota(jnp.int32, (bins_y, LANES), 0).astype(f32)
     bf16 = jnp.bfloat16
 
-    def product(t, side_of, first, spots, offset, count):
+    def operands(t, side_of, first, spots, offset, count):
         mine = lax.rem(lax.rem(gx + (side_of + (ngx - 1)), ngx) * ngy + gy, per)
         tile = gathered(t, side_of, mine)
         number = tile[6:7]
@@ -612,9 +610,13 @@
         rh = jnp.concatenate([jnp.where(layer == n, fh, 0.0) for n in range(bins_z)], axis=0)
         rl = jnp.concatenate([jnp.where(layer == n, fl, 0.0) for n in range(bins_z)], axis=0)
         rh, rl = rh.astype(bf16), rl.astype(bf16)
+        return [lh, lh, ll], [rh, rl, rh]
+
+    def product(ts, *rest):
+        pairs = [operands(t, *rest) for t in ts]
         return lax.dot_general(
-            jnp.concatenate([lh, lh, ll], axis=1),
-            jnp.concatenate([rh, rl, rh], axis=1),
+            jnp.concatenate([v for left, _ in pairs for v in left], axis=1),
+            jnp.concatenate([v for _, right in pairs for v in right], axis=1),
             (((1,), (1,)), ((), ())),
             preferred_element_type=f32,
         )
@@ -622,14 +624,19 @@
     far = lax.div(2 * gx, ngx)
 
     with jax.named_scope("p_force"):
-        @pl.loop(0, tiles)
-        def _(n):
-            near = (1 - lax.div(n + 2, tiles)) * (n + 1) + lax.div(n + 1, tiles) * (tiles - 1)
-            t = near + far * (tiles - 1 - n - near)
-            arrived = bead_recv.at[pl.ds(t * per, per)]
-            pltpu.make_async_copy(arrived, arrived, tile_sem.at[t]).wait()
-
-            value = product(t, 1, row_i, own_rows, 0.0, 4)
+        span = 2 if tiles % 2 == 0 else 1
+
+        @pl.loop(0, tiles // span)
+        def _(step):
+            ts = []
+            for k in range(span):
+                n = step * span + k
+                near = (1 - lax.div(n + 2, tiles)) * (n + 1) + lax.div(n + 1, tiles) * (tiles - 1)
+                t = near + far * (tiles - 1 - n - near)
+                arrived = bead_recv.at[pl.ds(t * per, per)]
+                pltpu.make_async_copy(arrived, arrived, tile_sem.at[t]).wait()
+                ts.append(t)
+            value = product(ts, 1, row_i, own_rows, 0.0, 4)
             for d in range(3):
                 for i in range(2):
                     for j in range(2):
@@ -640,7 +647,7 @@
 
             for h in range(2):
                 first = float(1 - h)
-                value = product(t, 2 * h, first, side_rows, first * (bins_xy - bins_y), 2)
+                value = product(ts, 2 * h, first, side_rows, first * (bins_xy - bins_y), 2)
                 for d in range(3):
                     for j in range(2):
                         start = (d * 2 + j) * bins_y

time: 16.2 us -> 16 us (0.988)
  Pallas kernels: 15.3 us -> 15.1 us
    pallas_call x1, Pallas kernels: 14.1 us -> 14 us  [local(): pl.pallas_call(functools.partial(kernel, sizes, slots), out_shape=[jax.Sh...]
where the time goes in v5:
time: 16 us; the launch traced here: 15.8 us
  Pallas kernels  15.1 us (94%)
  between operations  0.64 us (4%)
    pallas_call x1, Pallas kernels, local(): pl.pallas_call(functools.partial(kernel, sizes, slots), out_shape=[jax.Sh...  14 us
    pallas_call x1, Pallas kernels, local(): pl.pallas_call(functools.partial(finish, nx), out_shape=[jax.ShapeDtypeSt...  1.2 us

profile of v5, /device:TPU:0, one launch (start us, length us, event | category | flops | bytes accessed | tf_op | source)
XLA Modules:
  0.0 15.8 jit_solution(5809878176353261734)
XLA Ops:
  0.6 14.0 %shard_map.77 = (f32[19,128,128]{2,1,0:T(8,128)S(1)}, f32[2,16,128]{2,1,0:T(8,128)S(1)}, f32[19,4,8,64]{3,2,1,0:T(8,128)S(1)}) custom-call(f32[19,128,128]{2,1,0:T(8,128)} %bitcast.4, f32[19,4,8,64]{3,2,1,0:T(8,128)} %cpop_in.1, s32[8,16,128]{2,1,0:T(8,128)} %fmask_in.1, s32[4,8,64]{2,1,0:T(8,128)} %cmask_in.1, f32[24,128]{1,0:T(8,128)} %bitcast.5, ...), custom_call_target="tpu_custom_call" | custom-call | tf_op jit(solution)/shard_map/pallas_call | solution.py:828
  14.6 1.2 %shard_map.78 = (f32[19,128,128]{2,1,0:T(8,128)}, f32[19,4,8,64]{3,2,1,0:T(8,128)}) custom-call(f32[19,128,128]{2,1,0:T(8,128)S(1)} %get-tuple-element.7.fine, f32[2,16,128]{2,1,0:T(8,128)S(1)} %get-tuple-element.8.columns, f32[19,4,8,64]{3,2,1,0:T(8,128)S(1)} %get-tuple-element.9.coarse), custom_call_target="tpu_custom_call" | custom-call | tf_op jit(solution)/shard_map/pallas_call | solution.py:854

commit v6 on v5

--- a/solution.py
+++ b/solution.py
@@ -25,7 +25,10 @@
 SIGNS = (1, -1)
 FACE = {(a, s): [i for i in range(19) if VELOCITIES[i][a] == s] for a in range(3) for s in SIGNS}
 EDGES = [i for i in range(7, 19)]
-EDGES_YZ = [i for i in EDGES if not VELOCITIES[i][0]]
+
+
+def corner_messages(ngz):
+    return (1,) if ngz == 2 else SIGNS
 
 
 def along(vector, c):
@@ -198,12 +201,12 @@
     _, height, nz = fine.shape
     ny = height // nx
     turned = [5, 6, *range(11, 19)]
-    parts = [(coarse, coarse_out), (fine.at[0:5], fine_out.at[0:5]), (fine.at[7:11], fine_out.at[7:11])]
-    for n in range(0, 10, 2):
-        parts.append((target.at[n : n + 2], fine_out.at[turned[n] : turned[n] + 2]))
-    stores = [pltpu.make_async_copy(src, dst, store_sem.at[n]) for n, (src, dst) in enumerate(parts)]
-    for store in stores[:3]:
-        store.start()
+    def store(src, dst, n):
+        return pltpu.make_async_copy(src, dst, store_sem.at[n])
+
+    for low, high in ((0, 5), (7, 11)):
+        store(fine.at[low:high], fine_out.at[low:high], 0).start()
+    store(coarse, coarse_out, 1).start()
     last = lax.broadcasted_iota(jnp.int32, (ny, nz), 1)
     row = lax.broadcasted_iota(jnp.int32, (ny, nz), 0)
     for n, i in enumerate(turned):
@@ -218,9 +221,10 @@
                 spot, column[:, k : k + 1], fine[i, x * ny : (x + 1) * ny, :]
             )
         if n % 2:
-            stores[3 + n // 2].start()
-    for store in stores:
-        store.wait()
+            store(target.at[n - 1 : n + 1], fine_out.at[i - 1 : i + 1], 2).start()
+    store(fine.at[0:9], fine_out.at[0:9], 0).wait()
+    store(coarse, coarse_out, 1).wait()
+    store(target, fine_out.at[0:10], 2).wait()
 
 
 def repeat(count, act, most=8):
@@ -236,9 +240,9 @@
     stream, fzr, cstream,
     pops, cpops, fmask, cmask, bead_ref, bins_ref, tall,
     force, halo_force, halo_send, halo_recv, brim_send, brim_recv,
-    bead_rows, bead_send, bead_recv, fys, fzs, fxs, fxr, cxs, cys, czs, ces,
-    fyr, fer, cxr, cyr, czr, cer,
-    in_sem, bead_sem, tile_sem, ready_sem, cross_sem, send_sem, recv_sem,
+    bead_rows, bead_send, bead_recv, fys, fzs, cxs, cys, czs, ces,
+    fyr, cxr, cyr, czr, cer,
+    own_sem, bead_sem, tile_sem, ready_sem, cross_sem, recv_sem,
 ):
     ngx, ngy, ngz = sizes
     gx, gy, gz = lax.axis_index("gx"), lax.axis_index("gy"), lax.axis_index("gz")
@@ -270,7 +274,7 @@
         return pop_in.at[:, pl.ds(x * ny, w * ny)], pops.at[:, pl.ds(x * ny, w * ny)]
 
     loads = [
-        pltpu.make_async_copy(src, dst, in_sem.at[n])
+        pltpu.make_async_copy(src, dst, own_sem.at[n])
         for n, src, dst in (
             (0, bead_in, bead_ref), (1, bins_in, bins_ref), (2, *part(0, 2)), (2, *part(nx - 2, 2)),
             (3, cmask_in, cmask), (4, fmask_in, fmask), (5, cpop_in, cpops),
@@ -444,7 +448,7 @@
                 pops[q, at] = jnp.where(kept, pops[q, at], tall[q])
 
     with jax.named_scope("p_ends"):
-        pltpu.make_async_copy(*part(0, 4), in_sem.at[2]).wait()
+        pltpu.make_async_copy(*part(0, 4), own_sem.at[2]).wait()
         for load in loads[4:7]:
             load.wait()
         pl.loop(0, 2)(lambda n: prepare(n * (hx - 1)))
@@ -459,16 +463,16 @@
                 for n, value in enumerate([rho, *m, p[VELOCITIES.index((s, t, 0))]]):
                     brim_send[slot_of(s), slot_of(t), n : n + 1, :] = value[y : y + 1]
 
-    BRIM, HALO, COARSE_X, COARSE_Y, COARSE_Z, COARSE_EDGE, ROWS, CORNERS, ENDS, COLUMNS = range(10)
+    BRIM, HALO, COARSE_X, COARSE_Y, COARSE_Z, COARSE_EDGE, CROSS_Y, COLUMNS = range(8)
     buffers = [
         (brim_send, brim_recv), (halo_send, halo_recv),
         (cxs, cxr), (cys, cyr), (czs, czr), (ces, cer),
-        (fys, fyr), (fer, fer), (fxs, fxr), (fzs, fzr),
+        (fys, fyr), (fzs, fzr),
     ]
 
     def move(kind, src, dst, where):
         return pltpu.make_async_remote_copy(
-            src_ref=src, dst_ref=dst, send_sem=send_sem.at[kind], recv_sem=recv_sem.at[kind],
+            src_ref=src, dst_ref=dst, send_sem=own_sem.at[kind], recv_sem=recv_sem.at[kind],
             device_id=where, device_id_type=MESH,
         )
 
@@ -487,7 +491,7 @@
     def leave(*kinds):
         for kind in kinds:
             src = buffers[kind][0]
-            pltpu.make_async_copy(src, src, send_sem.at[kind]).wait()
+            pltpu.make_async_copy(src, src, own_sem.at[kind]).wait()
 
     def send_ends(kind, later, signs=SIGNS):
         for s in signs:
@@ -671,12 +675,15 @@
         return setup(rho, u, 1.0 / TAU_FINE, f, 1.0 - 0.5 / TAU_FINE)
 
     keep = 1.0 - 1.0 / TAU_FINE
+    lane_x = lax.broadcasted_iota(jnp.int32, (nx, nz), 1)
+    corner_signs = corner_messages(ngz)
 
     def rows(n):
         sign = (1 - 2 * n).astype(f32)
         y = (ny - 1) * (1 - n)
         p = [pops[i, rows_at(y), :] for i in range(19)]
         made = made_of(*moments(p), [force[d, rows_at(y), :] for d in range(3)])
+        turned = {}
         for j, i in enumerate(FACE[1, 1]):
             c = VELOCITIES[i]
             other = FACE[1, -1][j]
@@ -687,15 +694,16 @@
             if c[0]:
                 block = pltpu.roll(block, (1 if c[0] > 0 else nx - 1) + n * (c[0] * (nx - 2)), 0)
             fys[n, j] = block
-        where = (gx, lax.rem(gy + (1 - 2 * n) + ngy, ngy), gz)
-        move(ROWS, fys.at[n], fyr.at[n], where).start()
+            turned[c[2]] = block
+        y = lax.rem(gy + (1 - 2 * n) + ngy, ngy)
+        move(CROSS_Y, fys.at[n, 0:5], fyr.at[n, 0:5], (gx, y, gz)).start()
+        for q, s in enumerate(corner_signs):
+            fys[n, 6 + q] = jnp.where((lane_x == 0) == (n == 0), turned[1], turned[-1])
+            z = lax.rem(gz + (s + ngz), ngz)
+            move(CROSS_Y, fys.at[n, 6 + q], fyr.at[n, 6 + q], (gx, y, z)).start()
 
     with jax.named_scope("p_rows"):
         pl.loop(0, 2)(rows)
-        for n, i in enumerate(EDGES_YZ):
-            s = VELOCITIES[i][1]
-            block = fys.at[slot_of(s), FACE[1, s].index(i)]
-            plan(CORNERS, block, fer.at[n], VELOCITIES[i]).start()
 
     def end_rows(n):
         sign = (1 - 2 * n).astype(f32)
@@ -710,7 +718,7 @@
             straight = n == h
             even = jnp.where(straight, both[0][0], both[1][0])
             odd = jnp.where(straight, both[0][1], both[1][1])
-            fxs[n, h : h + 1, :] = keep * brim_recv[h, n, 4:5, :] + (even + sign * odd)
+            fys[n, 5, h : h + 1, :] = keep * brim_recv[h, n, 4:5, :] + (even + sign * odd)
 
     with jax.named_scope("p_hwait"):
         arrive(BRIM)
@@ -718,7 +726,8 @@
     with jax.named_scope("p_endrows"):
         pl.loop(0, 2)(end_rows)
         for s in SIGNS:
-            send(ENDS, slot_of(s), (0, s, 0))
+            n = slot_of(s)
+            plan(CROSS_Y, fys.at[n, 5], fyr.at[n, 5], (0, s, 0)).start()
 
     def collide(p, rho, m, f, x):
         post = collided(p, rho, m, f)
@@ -769,7 +778,7 @@
         fill_coarse(cstream, cxr, cyr, czr, cer)
 
     with jax.named_scope("p_ywait"):
-        arrive(ROWS, CORNERS, ENDS)
+        arrive(CROSS_Y)
 
     with jax.named_scope("p_yfill"):
         corner = lax.broadcasted_iota(jnp.int32, (nx, nz), 1)
@@ -779,10 +788,11 @@
                 c = VELOCITIES[i]
                 block = fyr[slot_of(s), j]
                 if c[2]:
-                    block = jnp.where(corner == side(c[2], nz), fer[EDGES_YZ.index(i)], block)
+                    q = corner_signs.index(c[2]) if c[2] in corner_signs else 0
+                    block = jnp.where(corner == side(c[2], nz), fyr[slot_of(s), 6 + q], block)
                 if c[0]:
                     h = slot_of(c[0])
-                    end = fxr[slot_of(s), h : h + 1, :]
+                    end = fyr[slot_of(s), 5, h : h + 1, :]
                     block = jnp.where(row_x == side(c[0], nx), end, block)
                 stream[i, rows_at(side(s, ny)), :] = block
 
@@ -792,7 +802,7 @@
     with jax.named_scope("p_final"):
         sent = bead_recv.at[pl.ds(0, owners - 1)]
         pltpu.make_async_copy(sent, sent, bead_sem).wait()
-        leave(*range(10))
+        leave(*range(8))
 
 
 def local(populations, coarse_pops, fine_mask, coarse_mask, bead_data, bead_bins):
@@ -813,14 +823,14 @@
     vmem_spec = pl.BlockSpec(memory_space=pltpu.VMEM)
     dma = pltpu.SemaphoreType.DMA
 
-    fine_rim = [(2, 5, nx, nz), (2, ny, LANES), (len(EDGES_YZ), nx, nz)]
+    cross_y = (2, 6 + len(corner_messages(sizes[2])), nx, nz)
     coarse_rim = [(2, 5, hy, hz), (2, 5 * hx, 1, hz), (2, hy, LANES), (12, 1, LANES)]
     shapes = [(19, nx * ny, nz), (2, ny, LANES), coarse_pops.shape]
     vmem = [
         (3, nx * ny, nz), (2, 3, ny, nz),
         (2, 9, ny, nz), (2, 9, ny, nz), (2, 2, 8, nz), (2, 2, 8, nz),
         (FIELDS, LANES), (sizes[1], sizes[0] + 2, rows, LANES), (owners, 3, rows, LANES),
-        *fine_rim[:2], (2, 2, nz), (2, 2, nz), *coarse_rim, fine_rim[0], fine_rim[2], *coarse_rim,
+        cross_y, (2, ny, LANES), *coarse_rim, cross_y, *coarse_rim,
     ]
     operands = (
         populations.reshape(19, nx * ny, nz), coarse_pops, fine_mask, coarse_mask, beads, bins
@@ -839,13 +849,12 @@
             pltpu.VMEM((chunks, LANES), i32),
             pltpu.VMEM((19, ny, nz), f32),
             *[pltpu.VMEM(shape, f32) for shape in vmem],
-            dma((7,)),
+            dma((8,)),
             dma,
             dma((owners // per,)),
             pltpu.SemaphoreType.REGULAR((owners // per,)),
             pltpu.SemaphoreType.REGULAR,
-            dma((10,)),
-            dma((10,)),
+            dma((8,)),
         ],
         compiler_params=pltpu.CompilerParams(
             collective_id=0, has_side_effects=True, vmem_limit_bytes=LIMIT
@@ -856,7 +865,7 @@
         out_shape=[jax.ShapeDtypeStruct(shape, f32) for shape in (shapes[0], shapes[2])],
         in_specs=[vmem_spec] * 3,
         out_specs=[any_spec] * 2,
-        scratch_shapes=[pltpu.VMEM((10, nx * ny, nz), f32), dma((8,))],
+        scratch_shapes=[pltpu.VMEM((10, nx * ny, nz), f32), dma((3,))],
         compiler_params=pltpu.CompilerParams(vmem_limit_bytes=LIMIT),
     )(fine, columns, coarse)
     return fine.reshape(populations.shape), coarse

time: 16 us -> 15.8 us (0.988)
  Pallas kernels: 15.1 us -> 14.9 us
    pallas_call x1, Pallas kernels: 14 us -> 13.8 us  [local(): pl.pallas_call(functools.partial(kernel, sizes, slots), out_shape=[jax.Sh...]
where the time goes in v6:
time: 15.8 us; the launch traced here: 15.6 us
  Pallas kernels  14.9 us (94%)
  between operations  0.64 us (4%)
    pallas_call x1, Pallas kernels, local(): pl.pallas_call(functools.partial(kernel, sizes, slots), out_shape=[jax.Sh...  13.8 us
    pallas_call x1, Pallas kernels, local(): pl.pallas_call(functools.partial(finish, nx), out_shape=[jax.ShapeDtypeSt...  1.15 us

profile of v6, /device:TPU:0, one launch (start us, length us, event | category | flops | bytes accessed | tf_op | source)
XLA Modules:
  0.0 15.6 jit_solution(1353994476210713663)
XLA Ops:
  0.6 13.8 %shard_map.77 = (f32[19,128,128]{2,1,0:T(8,128)S(1)}, f32[2,16,128]{2,1,0:T(8,128)S(1)}, f32[19,4,8,64]{3,2,1,0:T(8,128)S(1)}) custom-call(f32[19,128,128]{2,1,0:T(8,128)} %bitcast.4, f32[19,4,8,64]{3,2,1,0:T(8,128)} %cpop_in.1, s32[8,16,128]{2,1,0:T(8,128)} %fmask_in.1, s32[4,8,64]{2,1,0:T(8,128)} %cmask_in.1, f32[24,128]{1,0:T(8,128)} %bitcast.5, ...), custom_call_target="tpu_custom_call" | custom-call | tf_op jit(solution)/shard_map/pallas_call | solution.py:838
  14.4 1.2 %shard_map.78 = (f32[19,128,128]{2,1,0:T(8,128)}, f32[19,4,8,64]{3,2,1,0:T(8,128)}) custom-call(f32[19,128,128]{2,1,0:T(8,128)S(1)} %get-tuple-element.7.fine, f32[2,16,128]{2,1,0:T(8,128)S(1)} %get-tuple-element.8.columns, f32[19,4,8,64]{3,2,1,0:T(8,128)S(1)} %get-tuple-element.9.coarse), custom_call_target="tpu_custom_call" | custom-call | tf_op jit(solution)/shard_map/pallas_call | solution.py:863

commit v7 on v6

--- a/solution.py
+++ b/solution.py
@@ -521,7 +521,8 @@
         def _():
             pl.semaphore_wait(barrier, owners - 1 + lower)
             loop(0, me, send_beads)
-            loop(me + 1, owners, send_beads)
+            loop(me + 1, heads, send_beads)
+            loop(0, owners - heads, lambda n: send_beads(owners - 1 - n))
             reply_cross()
             send_ends(BRIM, later=False)
             send_ends(HALO, later=False)

time: 15.8 us -> 15.8 us (level)
  no operation moved by 1% of the time
where the time goes in v7:
time: 15.8 us; the launch traced here: 15.6 us
  Pallas kernels  14.9 us (94%)
  between operations  0.64 us (4%)
    pallas_call x1, Pallas kernels, local(): pl.pallas_call(functools.partial(kernel, sizes, slots), out_shape=[jax.Sh...  13.8 us
    pallas_call x1, Pallas kernels, local(): pl.pallas_call(functools.partial(finish, nx), out_shape=[jax.ShapeDtypeSt...  1.15 us

profile of v7, /device:TPU:0, one launch (start us, length us, event | category | flops | bytes accessed | tf_op | source)
XLA Modules:
  0.0 15.6 jit_solution(13717776630698164363)
XLA Ops:
  0.6 13.8 %shard_map.77 = (f32[19,128,128]{2,1,0:T(8,128)S(1)}, f32[2,16,128]{2,1,0:T(8,128)S(1)}, f32[19,4,8,64]{3,2,1,0:T(8,128)S(1)}) custom-call(f32[19,128,128]{2,1,0:T(8,128)} %bitcast.4, f32[19,4,8,64]{3,2,1,0:T(8,128)} %cpop_in.1, s32[8,16,128]{2,1,0:T(8,128)} %fmask_in.1, s32[4,8,64]{2,1,0:T(8,128)} %cmask_in.1, f32[24,128]{1,0:T(8,128)} %bitcast.5, ...), custom_call_target="tpu_custom_call" | custom-call | tf_op jit(solution)/shard_map/pallas_call | solution.py:839
  14.4 1.2 %shard_map.78 = (f32[19,128,128]{2,1,0:T(8,128)}, f32[19,4,8,64]{3,2,1,0:T(8,128)}) custom-call(f32[19,128,128]{2,1,0:T(8,128)S(1)} %get-tuple-element.7.fine, f32[2,16,128]{2,1,0:T(8,128)S(1)} %get-tuple-element.8.columns, f32[19,4,8,64]{3,2,1,0:T(8,128)S(1)} %get-tuple-element.9.coarse), custom_call_target="tpu_custom_call" | custom-call | tf_op jit(solution)/shard_map/pallas_call | solution.py:864

commit v8 on v7

--- a/solution.py
+++ b/solution.py
@@ -538,6 +538,7 @@
             pl.semaphore_wait(cross_sem, len(cross) - lower)
 
     with jax.named_scope("p_csend"):
+        send_ends(HALO, later=True, signs=(1,))
         pack_x(cstream, cxs, ces)
         for s in SIGNS:
             send(COARSE_X, slot_of(s), (s, 0, 0))
@@ -549,7 +550,6 @@
             send(COARSE_EDGE, n, VELOCITIES[i])
         for n in range(2):
             fzs[n] = jnp.zeros((ny, LANES), f32)
-        send_ends(HALO, later=True, signs=(1,))
         force[...] = jnp.zeros_like(force)
         halo_force[...] = jnp.zeros_like(halo_force)
 

time: 15.8 us -> 15.8 us (level)
  no operation moved by 1% of the time
where the time goes in v8:
time: 15.8 us; the launch traced here: 15.6 us
  Pallas kernels  14.9 us (94%)
  between operations  0.64 us (4%)
    pallas_call x1, Pallas kernels, local(): pl.pallas_call(functools.partial(kernel, sizes, slots), out_shape=[jax.Sh...  13.8 us
    pallas_call x1, Pallas kernels, local(): pl.pallas_call(functools.partial(finish, nx), out_shape=[jax.ShapeDtypeSt...  1.15 us

profile of v8, /device:TPU:0, one launch (start us, length us, event | category | flops | bytes accessed | tf_op | source)
XLA Modules:
  0.0 15.6 jit_solution(4163337688370053987)
XLA Ops:
  0.6 13.8 %shard_map.77 = (f32[19,128,128]{2,1,0:T(8,128)S(1)}, f32[2,16,128]{2,1,0:T(8,128)S(1)}, f32[19,4,8,64]{3,2,1,0:T(8,128)S(1)}) custom-call(f32[19,128,128]{2,1,0:T(8,128)} %bitcast.4, f32[19,4,8,64]{3,2,1,0:T(8,128)} %cpop_in.1, s32[8,16,128]{2,1,0:T(8,128)} %fmask_in.1, s32[4,8,64]{2,1,0:T(8,128)} %cmask_in.1, f32[24,128]{1,0:T(8,128)} %bitcast.5, ...), custom_call_target="tpu_custom_call" | custom-call | tf_op jit(solution)/shard_map/pallas_call | solution.py:839
  14.4 1.2 %shard_map.78 = (f32[19,128,128]{2,1,0:T(8,128)}, f32[19,4,8,64]{3,2,1,0:T(8,128)}) custom-call(f32[19,128,128]{2,1,0:T(8,128)S(1)} %get-tuple-element.7.fine, f32[2,16,128]{2,1,0:T(8,128)S(1)} %get-tuple-element.8.columns, f32[19,4,8,64]{3,2,1,0:T(8,128)S(1)} %get-tuple-element.9.coarse), custom_call_target="tpu_custom_call" | custom-call | tf_op jit(solution)/shard_map/pallas_call | solution.py:864
